TPU v7x, 256 devices: a whole 4x4x8 slice. The times are simulated.
256 devices in a mesh: dp: 8 (over z), ctx: 32 (over y, x, core).
Axes of the slice: x: 4, y: 4, z: 8, core: 2. Of those that a mesh axis runs over, the one named last changes fastest.
Arguments:
- queries: bfloat16 [65536, 256], P(('dp', 'ctx')), parts along dimension 0, may hold values from -64 to 64
- key_rows: bfloat16 [65536, 128], P(('dp', 'ctx')), parts along dimension 0, may hold values from -8 to 8
- value_rows: bfloat16 [65536, 128], P(('dp', 'ctx')), parts along dimension 0, may hold values from -6 to 6
- grad_output: bfloat16 [65536, 256], P(('dp', 'ctx')), parts along dimension 0, may hold values from -6 to 6
- doc_lengths: int32 [128], P('dp'), parts along dimension 0, may hold values from 1 to 2048, 8192 in all
- block_order: int32 [512], P('dp'), parts along dimension 0, may hold values from 0 to 63, each once
Outputs:
- attention: bfloat16 [65536, 256], P(('dp', 'ctx')), parts along dimension 0
- grad_queries: bfloat16 [65536, 256], P(('dp', 'ctx')), parts along dimension 0
- grad_keys: bfloat16 [65536, 128], P(('dp', 'ctx')), parts along dimension 0
- grad_values: bfloat16 [65536, 128], P(('dp', 'ctx')), parts along dimension 0
There are 8 independent parts, one for each index of `dp`. A program takes and returns all parts, laid end to end along the dimension named above; each array names one. Nothing has to cross between parts.
Inputs may be any that keep to these rules, and one draw needn't show every extreme that they name: `doc_lengths`: 16 lengths summing to 8192, the longest exactly 2048. `block_order`: each of the 64 block numbers once.
All inputs are finite; a program needn't handle non-finite values.
Results may differ from a plain program's by a relative error of at most 0.035.
Values may be sent and summed in bfloat16 or wider, within the bound.
No kernel may reach another device: no remote copies, remote signals or barrier semaphores. Data moves between devices by JAX's collectives and lax.ppermute only.
A program may use at most 64 MiB of HBM per device.

v0:
```python
import jax
import jax.numpy as jnp
from jax import lax
from jax.sharding import PartitionSpec as P

BLK = 128


NEG = -1e30


def locate(block_order, first, count):
    rows = first + jnp.arange(count, dtype=jnp.int32)
    which = rows // BLK
    table = jnp.arange(block_order.shape[0], dtype=jnp.int32)
    picked = jnp.sum(jnp.where(which[:, None] == table[None, :], block_order[None, :], 0), axis=1)
    return picked * BLK + rows % BLK


def doc_index(ends, places):
    return jnp.sum((ends[None, :] <= places[:, None]).astype(jnp.int32), axis=1)


def masked_scores(qry, qpos, qdoc, kys, kpos, kdoc, scale):
    raw = jnp.einsum("qhd,kd->hqk", qry, kys, preferred_element_type=jnp.float32) * scale
    allowed = (qdoc[:, None] == kdoc[None, :]) & (kpos[None, :] <= qpos[:, None])
    return (raw, allowed)


def grad_terms(qry, gout, logsum, delta, qpos, qdoc, kys, vals, kpos, kdoc, scale):
    raw, allowed = masked_scores(qry, qpos, qdoc, kys, kpos, kdoc, scale)
    prob = jnp.where(allowed, jnp.exp(raw - logsum[..., None]), 0.0)
    weights = prob.astype(jnp.bfloat16)
    dprob = jnp.einsum("qhd,kd->hqk", gout, vals, preferred_element_type=jnp.float32)
    dscore = (prob * (dprob - delta[..., None]) * scale).astype(jnp.bfloat16)
    grad_q = jnp.einsum("hqk,kd->qhd", dscore, kys, preferred_element_type=jnp.float32)
    grad_k = jnp.einsum("hqk,qhd->kd", dscore, qry, preferred_element_type=jnp.float32)
    grad_v = jnp.einsum("hqk,qhd->kd", weights, gout, preferred_element_type=jnp.float32)
    return (grad_q, grad_k, grad_v)


def per_device(queries, key_rows, value_rows, grad_output, doc_lengths, block_order):
    tokens = queries.shape[0]
    width = key_rows.shape[1]
    heads = queries.shape[1] // width
    scale = width ** (-0.5)
    ends = jnp.cumsum(doc_lengths)
    own_pos = locate(block_order, lax.axis_index("ctx") * tokens, tokens)
    own_doc = doc_index(ends, own_pos)
    all_keys, all_values = (
        lax.all_gather(key_rows, "ctx", axis=0, tiled=True),
        lax.all_gather(value_rows, "ctx", axis=0, tiled=True),
    )
    seq = all_keys.shape[0]
    all_pos = locate(block_order, 0, seq)
    all_doc = doc_index(ends, all_pos)
    span = min(seq, 2048)
    count_blocks = seq // span
    blocks = (
        all_keys.reshape(count_blocks, span, width),
        all_values.reshape(count_blocks, span, width),
        all_pos.reshape(count_blocks, span),
        all_doc.reshape(count_blocks, span),
    )
    query_heads = queries.reshape(tokens, heads, width)
    grad_heads = grad_output.reshape(tokens, heads, width)

    def stats_step(carry, block):
        top, total = carry
        kys, vals, kpos, kdoc = block
        raw, allowed = masked_scores(query_heads, own_pos, own_doc, kys, kpos, kdoc, scale)
        block_top = jnp.max(jnp.where(allowed, raw, NEG), axis=2)
        new_top = jnp.maximum(top, block_top)
        total = total * jnp.exp(top - new_top) + jnp.sum(
            jnp.where(allowed, jnp.exp(raw - new_top[..., None]), 0.0), axis=2
        )
        return ((new_top, total), None)

    start_top = jnp.full((heads, tokens), NEG, jnp.float32)
    start_total = jnp.zeros((heads, tokens), jnp.float32)
    (top, total), _ = lax.scan(stats_step, (start_top, start_total), blocks)
    logsum = top + jnp.log(total)

    def output_step(accum, block):
        kys, vals, kpos, kdoc = block
        raw, allowed = masked_scores(query_heads, own_pos, own_doc, kys, kpos, kdoc, scale)
        weights = jnp.where(allowed, jnp.exp(raw - logsum[..., None]), 0.0).astype(jnp.bfloat16)
        return (
            accum + jnp.einsum("hqk,kd->qhd", weights, vals, preferred_element_type=jnp.float32),
            None,
        )

    accum, _ = lax.scan(output_step, jnp.zeros((tokens, heads, width), jnp.float32), blocks)
    attention = accum.reshape(tokens, heads * width).astype(jnp.bfloat16)
    delta = jnp.sum(
        grad_heads.astype(jnp.float32)
        * attention.reshape(tokens, heads, width).astype(jnp.float32),
        axis=2,
    ).T
    zero_q = jnp.zeros((tokens, heads, width), jnp.float32)

    def key_step(grad_q, block):
        kys, vals, kpos, kdoc = block
        part_q, part_k, part_v = grad_terms(
            query_heads, grad_heads, logsum, delta, own_pos, own_doc, kys, vals, kpos, kdoc, scale
        )
        return (grad_q + part_q, (part_k, part_v))

    grad_q, (key_terms, value_terms) = lax.scan(key_step, zero_q, blocks)
    grad_k, grad_v = (
        lax.psum_scatter(key_terms.reshape(seq, width), "ctx", scatter_dimension=0, tiled=True),
        lax.psum_scatter(value_terms.reshape(seq, width), "ctx", scatter_dimension=0, tiled=True),
    )
    grad_queries = grad_q.reshape(tokens, heads * width).astype(jnp.bfloat16)
    return (attention, grad_queries, grad_k.astype(jnp.bfloat16), grad_v.astype(jnp.bfloat16))


def solution(mesh):
    placed = (
        P(("dp", "ctx"), None),
        P(("dp", "ctx"), None),
        P(("dp", "ctx"), None),
        P(("dp", "ctx"), None),
        P("dp"),
        P("dp"),
    )
    return jax.shard_map(
        per_device,
        mesh=mesh,
        in_specs=placed,
        out_specs=(
            P(("dp", "ctx"), None),
            P(("dp", "ctx"), None),
            P(("dp", "ctx"), None),
            P(("dp", "ctx"), None),
        ),
        check_vma=False,
    )
```

profile of v0, /device:TPU:160, one launch (start us, length us, event | category | flops | bytes accessed | tf_op | source)
XLA Modules:
  0.0 359.1 jit_solution(37139036626652673)
XLA Ops:
  7.2 0.7 all-gather.5.cloned.1.call-update
  7.9 0.7 all-gather.3.cloned.1.call-update
  8.8 0.7 select_reduce_fusion.1
  9.6 0.7 copy.33
  10.4 1.1 select_reduce_fusion
  11.6 0.2 convert_reduce_fusion
  11.9 1.0 copy.34
  13.0 1.0 copy.38
  14.1 46.2 %all-gather.5.cloned.1.call-done = bf16[8192,128]{1,0:T(8,128)(2,1)} async-done(((bf16[256,128]{1,0:T(8,128)(2,1)}), bf16[8192,128]{1,0:T(8,128)(2,1)}) %all-gather.5.cloned.1.call-update) | async-done | bytes 2097168 | tf_op jit(solution)/shard_map/all_gather | solution.py:51
  60.3 33.9 %while.39 = (s32[]{:T(128)}, f32[2,256]{1,0:T(2,128)S(1)}, f32[2,256]{1,0:T(2,128)S(1)}, s32[256]{0:T(256)S(1)}, s32[4,2048]{1,0:T(4,128)S(1)}, /*index=5*/s32[4...) while((s32[]{:T(128)}, f32[2,256]{1,0:T(2,128)S(1)}, ...), condition=%wide.region_8.9_spmd.clone, body=%wide.region_5.8_spmd.clone.sunk | while | flops 277350912 | bytes 10695292 | solution.py:81
  60.3 1.4 compare_and_fusion.6
  61.8 3.7 %fusion.89 = (f32[2,256]{1,0:T(2,128)S(1)}, f32[2048,256,2]{1,0,2:T(8,128)}) fusion(pred[256,2048]{0,1:T(8,128)(4,1)S(1)} %compare_and_fusion.6, bf16[256,2,128]{2,0,1:T(8,128)(2,1)S(1)} %get-tuple-element.701, bf16[4,2048,128]{2,1,0:T(8,128)(2,1)} %get-tuple-element.700, s32[]{:T(128)} %get-tuple-element.682), kind=kOutput, calls=%fused_computation.2.clone.1 | convolution fusion | flops 271580672 | bytes 5376512 | tf_op jit(solution)/shard_map/while/body/eval_jaxpr/qhd,kd->hqk/dot_general | solution.py:25
  65.5 3.2 fusion.91
  68.8 1.4 compare_and_fusion.6
  70.2 3.7 %fusion.89 = (f32[2,256]{1,0:T(2,128)S(1)}, f32[2048,256,2]{1,0,2:T(8,128)}) fusion(pred[256,2048]{0,1:T(8,128)(4,1)S(1)} %compare_and_fusion.6, bf16[256,2,128]{2,0,1:T(8,128)(2,1)S(1)} %get-tuple-element.701, bf16[4,2048,128]{2,1,0:T(8,128)(2,1)} %get-tuple-element.700, s32[]{:T(128)} %get-tuple-element.682), kind=kOutput, calls=%fused_computation.2.clone.1 | convolution fusion | flops 271580672 | bytes 5376512 | tf_op jit(solution)/shard_map/while/body/eval_jaxpr/qhd,kd->hqk/dot_general | solution.py:25
  74.0 3.2 fusion.91
  77.3 1.4 compare_and_fusion.6
  78.7 3.8 %fusion.89 = (f32[2,256]{1,0:T(2,128)S(1)}, f32[2048,256,2]{1,0,2:T(8,128)}) fusion(pred[256,2048]{0,1:T(8,128)(4,1)S(1)} %compare_and_fusion.6, bf16[256,2,128]{2,0,1:T(8,128)(2,1)S(1)} %get-tuple-element.701, bf16[4,2048,128]{2,1,0:T(8,128)(2,1)} %get-tuple-element.700, s32[]{:T(128)} %get-tuple-element.682), kind=kOutput, calls=%fused_computation.2.clone.1 | convolution fusion | flops 271580672 | bytes 5376512 | tf_op jit(solution)/shard_map/while/body/eval_jaxpr/qhd,kd->hqk/dot_general | solution.py:25
  82.5 3.2 fusion.91
  85.7 1.4 compare_and_fusion.6
  87.2 3.7 %fusion.89 = (f32[2,256]{1,0:T(2,128)S(1)}, f32[2048,256,2]{1,0,2:T(8,128)}) fusion(pred[256,2048]{0,1:T(8,128)(4,1)S(1)} %compare_and_fusion.6, bf16[256,2,128]{2,0,1:T(8,128)(2,1)S(1)} %get-tuple-element.701, bf16[4,2048,128]{2,1,0:T(8,128)(2,1)} %get-tuple-element.700, s32[]{:T(128)} %get-tuple-element.682), kind=kOutput, calls=%fused_computation.2.clone.1 | convolution fusion | flops 271580672 | bytes 5376512 | tf_op jit(solution)/shard_map/while/body/eval_jaxpr/qhd,kd->hqk/dot_general | solution.py:25
  90.9 3.2 fusion.91
  94.2 16.7 %all-gather.3.cloned.1.call-done = bf16[8192,128]{1,0:T(8,128)(2,1)} async-done(((bf16[256,128]{1,0:T(8,128)(2,1)}), bf16[8192,128]{1,0:T(8,128)(2,1)}) %all-gather.3.cloned.1.call-update) | async-done | bytes 2097168 | tf_op jit(solution)/shard_map/all_gather | solution.py:52
  110.9 16.2 %while.40 = (s32[]{:T(128)}, f32[256,2,128]{0,2,1:T(8,128)S(1)}, bf16[4,2048,128]{2,1,0:T(8,128)(2,1)}, s32[256]{0:T(256)S(1)}, s32[4,2048]{1,0:T(4,128)S(1)}, /...) while((s32[]{:T(128)}, f32[256,2,128]{0,2,1:T(8,128)S(1)}, ...), condition=%wide.region_10.11_spmd.clone, body=%wide.region_9.10_spmd.clone.sunk | while | flops 542769152 | bytes 2806915 | solution.py:93
  110.9 1.4 compare_and_fusion.7
  112.3 2.6 fusion.96
  114.9 1.4 compare_and_fusion.7
  116.4 2.5 fusion.96
  119.0 1.4 compare_and_fusion.7
  120.4 2.5 fusion.96
  123.0 1.4 compare_and_fusion.7
  124.5 2.5 fusion.96
  127.1 41.3 %while.41 = (s32[]{:T(128)}, f32[256,2,128]{0,2,1:T(8,128)S(1)}, f32[4,2048,128]{2,1,0:T(8,128)}, f32[4,2048,128]{2,1,0:T(8,128)}, bf16[4,2048,128]{2,1,0:T(8,12...) while((s32[]{:T(128)}, f32[256,2,128]{0,2,1:T(8,128)S(1)}, ...), condition=%wide.region_13.14_spmd.clone, body=%wide.region_12.13_spmd.clone.sunk | while | flops 1352269824 | bytes 24699556 | solution.py:109
  127.1 1.4 compare_and_fusion.8
  128.6 2.1 fusion.107
  130.7 1.8 fusion.108
  132.4 1.7 fusion.110
  134.1 1.7 fusion.111
  135.8 1.6 fusion.109
  137.4 1.4 compare_and_fusion.8
  138.9 2.1 fusion.107
  141.0 1.8 fusion.108
  142.7 1.7 fusion.110
  144.5 1.7 fusion.111
  146.2 1.6 fusion.109
  147.8 1.4 compare_and_fusion.8
  149.3 2.0 fusion.107
  151.3 1.8 fusion.108
  153.1 1.7 fusion.110
  154.8 1.7 fusion.111
  156.5 1.6 fusion.109
  158.1 1.4 compare_and_fusion.8
  159.6 2.1 fusion.107
  161.7 1.8 fusion.108
  163.4 1.7 fusion.110
  165.1 1.7 fusion.111
  166.8 1.6 fusion.109
  168.5 0.5 reduce-scatter.5.cloned.1.call-update
  169.0 0.8 copy.46
  169.8 0.8 copy.42
  170.6 87.3 %reduce-scatter.3.cloned.1.call-done = f32[256,128]{1,0:T(8,128)} async-done(((f32[8192,128]{1,0:T(8,128)}), f32[256,128]{1,0:T(8,128)}) %reduce-scatter.3.cloned.1.call-update) | async-done | bytes 131088 | tf_op jit(solution)/shard_map/reduce_scatter | solution.py:111
  257.9 1.5 convert_element_type.48
  259.4 91.6 %reduce-scatter.5.cloned.1.call-done = f32[256,128]{1,0:T(8,128)} async-done(((f32[8192,128]{1,0:T(8,128)}), f32[256,128]{1,0:T(8,128)}) %reduce-scatter.5.cloned.1.call-update) | async-done | bytes 131088 | tf_op jit(solution)/shard_map/reduce_scatter | solution.py:112
  351.0 1.5 convert_element_type.49
  (50 shorter events, 1.2 us)
Async XLA Ops:
  7.2 53.1 %all-gather.5.cloned.1.call-start = ((), (), s32[]{:S(2)}) async-start(), calls=%async_computation.3 | async-start | bytes 2162688 | tf_op jit(solution)/shard_map/all_gather | solution.py:51
  7.9 103.0 %all-gather.3.cloned.1.call-start = ((), (), s32[]{:S(2)}) async-start(), calls=%async_computation.2 | async-start | bytes 2162688 | tf_op jit(solution)/shard_map/all_gather | solution.py:52
  8.6 249.2 %reduce-scatter.3.cloned.1.call-start = ((), (), s32[]{:S(2)}) async-start(), calls=%async_computation.4 | async-start | bytes 4325376 | tf_op jit(solution)/shard_map/reduce_scatter | solution.py:111
  168.4 182.6 %reduce-scatter.5.cloned.1.call-start = ((), (), s32[]{:S(2)}) async-start(), calls=%async_computation.5 | async-start | bytes 4325376 | tf_op jit(solution)/shard_map/reduce_scatter | solution.py:112
Sparse Core Ops, SparseCore 0:
  10.5 49.7 all-gather.4
  62.8 47.9 all-gather.2
  168.6 89.2 reduce-scatter.2
  261.7 89.3 reduce-scatter.4
where the time goes:
time: 362 us; the launch traced here: 359 us
  waiting for transfers between devices  244 us (67%)
  matrix products  60.4 us (17%)
  other arithmetic  35.7 us (10%)
  between operations  13.9 us (4%)
  local copies, waits for them, and re-layouts  4.77 us (1%)
    reduce_scatter x1, waiting for transfers between devices, per_device(): lax.psum_scatter(value_terms.reshape(seq, width), 'ctx', scatter_dimensio...  91.6 us
    reduce_scatter x1, waiting for transfers between devices, per_device(): lax.psum_scatter(key_terms.reshape(seq, width), 'ctx', scatter_dimension=...  87.3 us
    all_gather x1, waiting for transfers between devices, per_device(): lax.all_gather(key_rows, 'ctx', axis=0, tiled=True)  46.2 us
    dot_general x8, matrix products, masked_scores(): jnp.einsum('qhd,kd->hqk', qry, kys, preferred_element_type=jnp.float32)  23.2 us
    and x12, other arithmetic, masked_scores(): (qdoc[:, None] == kdoc[None, :]) & (kpos[None, :] <= qpos[:, None])  17.4 us
    all_gather x1, waiting for transfers between devices, per_device(): lax.all_gather(value_rows, 'ctx', axis=0, tiled=True)  16.7 us
    reduce_sum x4, other arithmetic, stats_step(): jnp.sum(jnp.where(allowed, jnp.exp(raw - new_top[..., None]), 0.0), axis=2)  12.8 us
    dot_general x4, matrix products, output_step(): jnp.einsum('hqk,kd->qhd', weights, vals, preferred_element_type=jnp.float32)  10.2 us
  transfers between devices with their start and end apart: 4, of which 4 were waited for; matrix products, arithmetic and copies ran while one was open for 12% of the time, Pallas kernels for 0%

commit v1 on v0

v1 whole, which is shorter than its diff:
```python
import functools

import jax
import jax.numpy as jnp
from jax import lax
from jax.experimental import pallas as pl
from jax.experimental.pallas import tpu as pltpu
from jax.sharding import PartitionSpec as P

BLK = 128
HD = 128
NBLK = 64
NDOC = 16
SIDE = 4
CHUNK = 4
WINDOW = 20
NEG = -1e30
SCALE = HD**-0.5
LOG2E = 1.4426950408889634
SCALE2 = SCALE * LOG2E

NT = (((1,), (1,)), ((), ()))
NN = (((1,), (0,)), ((), ()))
TN = (((0,), (0,)), ((), ()))


def device_of(y, x, core):
    return (y % SIDE) * 2 * SIDE + (x % SIDE) * 2 + core


def along(axis_of_core):
    groups = []
    for core in range(2):
        for fixed in range(SIDE):
            if axis_of_core[core] == "y":
                groups.append([device_of(i, fixed, core) for i in range(SIDE)])
            else:
                groups.append([device_of(fixed, i, core) for i in range(SIDE)])
    return groups


FIRST = along("yx")
SECOND = along("xy")
SWAP = [(i, i ^ 1) for i in range(2 * SIDE * SIDE)]


def mm(a, b, dims):
    return lax.dot_general(a, b, dims, preferred_element_type=jnp.float32)


def attend(order, lengths, q_ref, g_ref, own_ref, oth_ref, o_ref, dq_ref, dkv_own, dkv_oth, kv, s_ref, acc, table):
    me = lax.axis_index("ctx")
    core = me % 2
    half = NBLK // 2

    def place(s, _):
        dev = s // 2
        y, x, c = dev // (2 * SIDE), (dev // 2) % SIDE, dev % 2
        slot = jnp.where(c == 0, x * SIDE + y, y * SIDE + x)
        plane = jnp.where(c == core, 0, 1)
        table[order[s]] = plane * half + slot * 2 + s % 2
        return 0

    lax.fori_loop(0, NBLK, place, 0)
    acc[...] = jnp.zeros_like(acc)
    kv[pl.ds(0, half * BLK), :] = own_ref[...]
    kv[pl.ds(half * BLK, half * BLK), :] = oth_ref[...]

    lane = lax.broadcasted_iota(jnp.int32, (1, 2 * BLK), 1) % BLK
    sub = lax.broadcasted_iota(jnp.int32, (BLK, 2 * BLK), 0)

    for i in range(2):
        blk = order[2 * me + i]
        qpos = blk * BLK + lane
        end, low = jnp.int32(0), jnp.int32(0)
        qstart = jnp.zeros((1, 2 * BLK), jnp.int32)
        for d in range(NDOC):
            end = end + lengths[d]
            qstart = jnp.where(qpos >= end, end, qstart)
            low = jnp.where(blk * BLK >= end, end, low)
        count = blk - low // BLK + 1
        trips = (count + CHUNK - 1) // CHUNK

        rows = pl.ds(i * BLK, BLK)
        qs = jnp.concatenate([q_ref[rows, :HD], q_ref[rows, HD:]], axis=0)
        gs = jnp.concatenate([g_ref[rows, :HD], g_ref[rows, HD:]], axis=0)

        def row_of(t, j):
            p = jnp.maximum(blk - (t * CHUNK + j), 0)
            return pl.multiple_of(table[p] * BLK, BLK)

        def load(t, cols):
            return jnp.concatenate([kv[pl.ds(row_of(t, j), BLK), cols] for j in range(CHUNK)], axis=0)

        keys, vals = slice(0, HD), slice(HD, 2 * HD)

        def scores(t, top):
            s = mm(load(t, keys), qs, NT)
            for j in range(CHUNK):
                kpos = (blk - (t * CHUNK + j)) * BLK + sub
                ok = (kpos >= qstart) & (kpos <= qpos)
                part = jnp.where(ok, s[j * BLK : (j + 1) * BLK], NEG)
                s_ref[pl.ds(pl.multiple_of((t * CHUNK + j) * BLK, BLK), BLK), :] = part
                top = jnp.maximum(top, jnp.max(part, axis=0, keepdims=True))
            return top

        top = lax.fori_loop(0, trips, scores, jnp.full((1, 2 * BLK), NEG, jnp.float32))

        def outputs(t, carry):
            total, out = carry
            at = pl.ds(pl.multiple_of(t * CHUNK * BLK, CHUNK * BLK), CHUNK * BLK)
            p = jnp.exp2((s_ref[at, :] - top) * SCALE2)
            s_ref[at, :] = p
            total = total + jnp.sum(p, axis=0, keepdims=True)
            out = out + mm(load(t, vals), p.astype(jnp.bfloat16), TN)
            return total, out

        total, out = lax.fori_loop(
            0, trips, outputs, (jnp.zeros((1, 2 * BLK), jnp.float32), jnp.zeros((HD, 2 * BLK), jnp.float32))
        )
        inv = 1.0 / total
        att = (out * inv).T.astype(jnp.bfloat16)
        o_ref[rows, :HD] = att[:BLK]
        o_ref[rows, HD:] = att[BLK:]
        prod = gs.astype(jnp.float32) * att.astype(jnp.float32)
        delta = jnp.sum(prod.T, axis=0, keepdims=True)

        def grads(t, dq):
            at = pl.ds(pl.multiple_of(t * CHUNK * BLK, CHUNK * BLK), CHUNK * BLK)
            p = s_ref[at, :] * inv
            dp = mm(load(t, vals), gs, NT)
            ds = (p * (dp - delta) * SCALE).astype(jnp.bfloat16)
            dv = mm(p.astype(jnp.bfloat16), gs, NN)
            dk = mm(ds, qs, NN)
            dq = dq + mm(load(t, keys), ds, TN)
            for j in range(CHUNK):
                to = pl.ds(row_of(t, j), BLK)
                acc[to, keys] += dk[j * BLK : (j + 1) * BLK]
                acc[to, vals] += dv[j * BLK : (j + 1) * BLK]
            return dq

        dq = lax.fori_loop(0, trips, grads, jnp.zeros((HD, 2 * BLK), jnp.float32)).T.astype(jnp.bfloat16)
        dq_ref[rows, :HD] = dq[:BLK]
        dq_ref[rows, HD:] = dq[BLK:]

    dkv_own[...] = acc[pl.ds(0, half * BLK), :].astype(jnp.bfloat16)
    dkv_oth[...] = acc[pl.ds(half * BLK, half * BLK), :].astype(jnp.bfloat16)


def attention_kernel(order, lengths, queries, grad, own, oth):
    tokens = queries.shape[0]
    rows = own.shape[0]
    vmem = pl.BlockSpec(memory_space=pltpu.VMEM)
    bf16 = jnp.bfloat16
    return pl.pallas_call(
        attend,
        out_shape=(
            jax.ShapeDtypeStruct((tokens, 2 * HD), bf16),
            jax.ShapeDtypeStruct((tokens, 2 * HD), bf16),
            jax.ShapeDtypeStruct((rows, 2 * HD), bf16),
            jax.ShapeDtypeStruct((rows, 2 * HD), bf16),
        ),
        in_specs=[pl.BlockSpec(memory_space=pltpu.SMEM)] * 2 + [vmem] * 4,
        out_specs=(vmem,) * 4,
        scratch_shapes=[
            pltpu.VMEM((2 * rows, 2 * HD), bf16),
            pltpu.VMEM((WINDOW * BLK, 2 * BLK), jnp.float32),
            pltpu.VMEM((2 * rows, 2 * HD), jnp.float32),
            pltpu.SMEM((NBLK,), jnp.int32),
        ],
        compiler_params=pltpu.CompilerParams(vmem_limit_bytes=50 * 1024 * 1024),
        name="attend",
    )(order, lengths, queries, grad, own, oth)


def per_device(queries, key_rows, value_rows, grad_output, doc_lengths, block_order):
    tokens = queries.shape[0]
    kv = jnp.concatenate([key_rows, value_rows], axis=1)
    line = lax.all_gather(kv, "ctx", axis=0, tiled=True, axis_index_groups=FIRST)
    spread = jnp.broadcast_to(line[None], (SIDE,) + line.shape)
    own = lax.all_to_all(spread, "ctx", 0, 0, tiled=True, axis_index_groups=SECOND)
    own = own.reshape(SIDE * SIDE * tokens, 2 * HD)
    oth = lax.ppermute(own, "ctx", SWAP)
    attention, grad_queries, dkv_own, dkv_oth = attention_kernel(
        block_order, doc_lengths, queries, grad_output, own, oth
    )
    back = lax.ppermute(dkv_oth, "ctx", SWAP)
    f32 = jnp.float32
    part = (dkv_own.astype(f32) + back.astype(f32)).astype(jnp.bfloat16)
    part = part.reshape(SIDE, SIDE * tokens, 2 * HD)
    part = lax.all_to_all(part, "ctx", 0, 0, tiled=True, axis_index_groups=SECOND)
    part = jnp.sum(part.astype(f32), axis=0).astype(jnp.bfloat16).reshape(SIDE, tokens, 2 * HD)
    part = lax.all_to_all(part, "ctx", 0, 0, tiled=True, axis_index_groups=FIRST)
    part = jnp.sum(part.astype(f32), axis=0).astype(jnp.bfloat16)
    return attention, grad_queries, part[:, :HD], part[:, HD:]


def solution(mesh):
    rows = P(("dp", "ctx"), None)
    return jax.shard_map(
        per_device,
        mesh=mesh,
        in_specs=(rows, rows, rows, rows, P("dp"), P("dp")),
        out_specs=(rows, rows, rows, rows),
        check_vma=False,
    )
```

time: 362 us -> 91.8 us (0.25)
  waiting for transfers between devices: 244 us -> 8.15 us
  blocking collectives: 0 us -> 66.4 us
  matrix products: 60.4 us -> 0 us
  other arithmetic: 35.7 us -> 2.21 us
  between operations: 13.9 us -> 0.69 us
  Pallas kernels: 0 us -> 9.81 us
    reduce_scatter x2 -> x0, waiting for transfers between devices: 179 us -> none  [the longest x1 91.6 us: per_device(): lax.psum_scatter(value_terms.reshape(seq, width), 'ctx', scatter_dimensio...]
    all_gather x2 -> x0, waiting for transfers between devices: 62.8 us -> none  [the longest x1 46.2 us: per_device(): lax.all_gather(key_rows, 'ctx', axis=0, tiled=True)]
    dot_general x28 -> x0, matrix products: 60.4 us -> none  [the longest x8 23.2 us: masked_scores(): jnp.einsum('qhd,kd->hqk', qry, kys, preferred_element_type=jnp.float32)]
    all_to_all x0 -> x3, blocking collectives: none -> 53.1 us  [the longest x1 20.7 us: per_device(): lax.all_to_all(spread, 'ctx', 0, 0, tiled=True, axis_index_groups=SECOND)]
    and x12 -> x0, other arithmetic: 17.4 us -> none  [masked_scores(): (qdoc[:, None] == kdoc[None, :]) & (kpos[None, :] <= qpos[:, None])]
    reduce_sum x9 -> x2, other arithmetic: 14.9 us -> 0.72 us  [the longest x1 0.64 us: per_device(): jnp.sum(part.astype(f32), axis=0).astype(jnp.bfloat16)]
    all_gather x0 -> x1, blocking collectives: none -> 13.3 us  [per_device(): lax.all_gather(kv, 'ctx', axis=0, tiled=True, axis_index_groups=FIRST)]
    pallas_call x0 -> x1, Pallas kernels: none -> 9.81 us  [attention_kernel(): pl.pallas_call(attend, out_shape=(jax.ShapeDtypeStruct((tokens, 2 * HD),...]
  transfers between devices with their start and end apart: 4 -> 2, of which waited for: 4 -> 2; matrix products, arithmetic and copies ran while one was open for 12% -> 0% of each run, Pallas kernels for 0% -> 0%
where the time goes in v1:
time: 91.8 us; the launch traced here: 91.5 us
  blocking collectives  66.4 us (72%)
  Pallas kernels  9.81 us (11%)
  waiting for transfers between devices  8.15 us (9%)
  other arithmetic  2.21 us (2%)
  local copies, waits for them, and re-layouts  2.13 us (2%)
  starting transfers between devices  2.09 us (2%)
    all_to_all x1, blocking collectives, per_device(): lax.all_to_all(spread, 'ctx', 0, 0, tiled=True, axis_index_groups=SECOND)  20.7 us
    all_to_all x1, blocking collectives, per_device(): lax.all_to_all(part, 'ctx', 0, 0, tiled=True, axis_index_groups=SECOND)  19 us
    all_to_all x1, blocking collectives, per_device(): lax.all_to_all(part, 'ctx', 0, 0, tiled=True, axis_index_groups=FIRST)  13.4 us
    all_gather x1, blocking collectives, per_device(): lax.all_gather(kv, 'ctx', axis=0, tiled=True, axis_index_groups=FIRST)  13.3 us
    pallas_call x1, Pallas kernels, attention_kernel(): pl.pallas_call(attend, out_shape=(jax.ShapeDtypeStruct((tokens, 2 * HD),...  9.81 us
    ppermute x1, waiting for transfers between devices, per_device(): oth = lax.ppermute(own, 'ctx', SWAP)  4.16 us
    ppermute x1, waiting for transfers between devices, per_device(): back = lax.ppermute(dkv_oth, 'ctx', SWAP)  4 us
    ppermute x1, starting transfers between devices, per_device(): back = lax.ppermute(dkv_oth, 'ctx', SWAP)  2.08 us
  transfers between devices with their start and end apart: 2, of which 2 were waited for; matrix products, arithmetic and copies ran while one was open for 0% of the time, Pallas kernels for 0%

profile of v1, /device:TPU:160, one launch (start us, length us, event | category | flops | bytes accessed | tf_op | source)
XLA Modules:
  0.0 91.5 jit_solution(593359927589737972)
XLA Ops:
  0.6 0.9 pad_maximum_fusion
  1.5 13.3 %all_gather.3 = bf16[1024,256]{1,0:T(8,128)(2,1)S(1)} all-gather(bf16[256,256]{1,0:T(8,128)(2,1)S(1)} %pad_maximum_fusion), channel_id=1, replica_groups={{0,8,16,24},{2,10,18,26},{4,12,20,28},{6,14,22,30},{1,3,5,7},{9,11,13,1..., dimensions={0}, use_global_device_ids=true | all-gather | bytes 655360 | tf_op jit(solution)/shard_map/all_gather | solution.py:179
  14.8 0.1 broadcast_in_dim.2
  15.0 0.0 copy-start
  15.0 0.0 copy-start.1
  15.0 0.0 copy-start.2
  15.0 0.0 copy-start.3
  15.0 20.7 %all_to_all.15 = bf16[4,1024,256]{2,1,0:T(8,128)(2,1)S(1)} all-to-all(bf16[4,1024,256]{2,1,0:T(8,128)(2,1)S(1)} %broadcast_in_dim.2), channel_id=1, replica_groups={{0,2,4,6},{8,10,12,14},{16,18,20,22},{24,26,28,30},{1,9,17,25},{3,11,19..., dimensions={0} | all-to-all | bytes 4194304 | tf_op jit(solution)/shard_map/all_to_all | solution.py:181
  35.8 0.0 copy-start.4
  35.8 0.0 collective-permute-start
  35.8 4.2 %collective-permute-done.oth_ref = bf16[4096,256]{1,0:T(8,128)(2,1)S(1)} collective-permute-done((bf16[4096,256]{1,0:T(8,128)(2,1)S(1)}, bf16[4096,256]{1,0:T(8,128)(2,1)S(1)}, u32[]{:S(2)}, u32[]{:S(2)}) %collective-permute-start) | collective-permute-done | bytes 2097184 | tf_op jit(solution)/shard_map/ppermute | solution.py:183
  39.9 0.0 copy-done.4
  39.9 0.0 copy-start.5
  39.9 1.3 %copy-done.5 = bf16[4096,256]{1,0:T(8,128)(2,1)} copy-done((bf16[4096,256]{1,0:T(8,128)(2,1)}, bf16[4096,256]{1,0:T(8,128)(2,1)S(1)}, u32[]{:S(2)}) %copy-start.5) | copy-done | bytes 2097176
  41.2 0.0 copy-done
  41.2 0.0 copy-done.1
  41.2 0.0 copy-done.2
  41.2 0.0 copy-done.3
  41.2 9.8 %attend.1 = (bf16[256,256]{1,0:T(8,128)(2,1)}, bf16[256,256]{1,0:T(8,128)(2,1)}, bf16[4096,256]{1,0:T(8,128)(2,1)S(1)}, bf16[4096,256]{1,0:T(8,128)(2,1)}) custom-call(s32[64]{0:T(128)S(1)} %copy-done.2, s32[16]{0:T(128)S(1)} %copy-done.3, bf16[256,256]{1,0:T(8,128)(2,1)S(1)} %copy-done, bf16[256,256]{1,0:T(8,128)(2,1)S(1)} %copy-done.1, ...), custom_call_target="tpu_custom_call" | custom-call | tf_op jit(solution)/shard_map/attend/pallas_call | solution.py:155
  51.0 2.1 %collective-permute-start.1 = (bf16[4096,256]{1,0:T(8,128)(2,1)}, bf16[4096,256]{1,0:T(8,128)(2,1)S(1)}, u32[]{:S(2)}, u32[]{:S(2)}) collective-permute-start(bf16[4096,256]{1,0:T(8,128)(2,1)} %get-tuple-element.11), channel_id=1, source_target_pairs={{0,1},{1,0},{2,3},{3,2},{4,5},{5,4},{6,7},{7,6},{8,9},{9,8},{10,11... | collective-permute-start | bytes 6291464 | tf_op jit(solution)/shard_map/ppermute | solution.py:187
  53.1 4.0 %collective-permute-done.1 = bf16[4096,256]{1,0:T(8,128)(2,1)S(1)} collective-permute-done((bf16[4096,256]{1,0:T(8,128)(2,1)}, bf16[4096,256]{1,0:T(8,128)(2,1)S(1)}, u32[]{:S(2)}, u32[]{:S(2)}) %collective-permute-start.1) | collective-permute-done | bytes 2097184 | tf_op jit(solution)/shard_map/ppermute | solution.py:187
  57.1 0.6 add_convert_fusion
  57.7 19.0 %all_to_all.16 = bf16[4,1024,256]{2,1,0:T(8,128)(2,1)S(1)} all-to-all(bf16[4,1024,256]{2,1,0:T(8,128)(2,1)S(1)} %bitcast.3), channel_id=1, replica_groups={{0,2,4,6},{8,10,12,14},{16,18,20,22},{24,26,28,30},{1,9,17,25},{3,11,19..., dimensions={0} | all-to-all | bytes 4194304 | tf_op jit(solution)/shard_map/all_to_all | solution.py:191
  76.7 0.6 reduce_sum.24
  77.4 13.4 %all_to_all.17 = bf16[4,256,256]{2,1,0:T(8,128)(2,1)S(1)} all-to-all(bf16[4,256,256]{2,1,0:T(8,128)(2,1)S(1)} %bitcast.6), channel_id=1, replica_groups={{0,8,16,24},{2,10,18,26},{4,12,20,28},{6,14,22,30},{1,3,5,7},{9,11,13,1..., dimensions={0} | all-to-all | bytes 1048576 | tf_op jit(solution)/shard_map/all_to_all | solution.py:193
  90.7 0.1 reduce_sum.25
  90.8 0.7 fusion
Async XLA Ops:
  15.0 26.3 %copy-start = (bf16[256,256]{1,0:T(8,128)(2,1)S(1)}, bf16[256,256]{1,0:T(8,128)(2,1)}, u32[]{:S(2)}) copy-start(bf16[256,256]{1,0:T(8,128)(2,1)} %q_ref.1) | copy-start | bytes 393220
  15.0 26.2 %copy-start.1 = (bf16[256,256]{1,0:T(8,128)(2,1)S(1)}, bf16[256,256]{1,0:T(8,128)(2,1)}, u32[]{:S(2)}) copy-start(bf16[256,256]{1,0:T(8,128)(2,1)} %g_ref.1) | copy-start | bytes 393220
  15.0 26.2 %copy-start.2 = (s32[64]{0:T(128)S(1)}, s32[64]{0:T(128)}, u32[]{:S(2)}) copy-start(s32[64]{0:T(128)} %order.1) | copy-start | bytes 772
  15.0 26.2 %copy-start.3 = (s32[16]{0:T(128)S(1)}, s32[16]{0:T(128)}, u32[]{:S(2)}) copy-start(s32[16]{0:T(128)} %lengths.1) | copy-start | bytes 196
  35.8 4.2 %copy-start.4 = (bf16[4,1024,256]{2,1,0:T(8,128)(2,1)}, bf16[4,1024,256]{2,1,0:T(8,128)(2,1)S(1)}, u32[]{:S(2)}) copy-start(bf16[4,1024,256]{2,1,0:T(8,128)(2,1)S(1)} %all_to_all.15) | copy-start | bytes 6291460
  35.8 4.2 %collective-permute-start = (bf16[4096,256]{1,0:T(8,128)(2,1)S(1)}, bf16[4096,256]{1,0:T(8,128)(2,1)S(1)}, u32[]{:S(2)}, u32[]{:S(2)}) collective-permute-start(bf16[4096,256]{1,0:T(8,128)(2,1)S(1)} %bitcast.4), channel_id=1, source_target_pairs={{0,1},{1,0},{2,3},{3,2},{4,5},{5,4},{6,7},{7,6},{8,9},{9,8},{10,11... | collective-permute-start | bytes 6291464 | tf_op jit(solution)/shard_map/ppermute | solution.py:183
  39.9 1.3 %copy-start.5 = (bf16[4096,256]{1,0:T(8,128)(2,1)}, bf16[4096,256]{1,0:T(8,128)(2,1)S(1)}, u32[]{:S(2)}) copy-start(bf16[4096,256]{1,0:T(8,128)(2,1)S(1)} %collective-permute-done.oth_ref) | copy-start | bytes 6291460
  51.0 6.1 %collective-permute-start.1 = (bf16[4096,256]{1,0:T(8,128)(2,1)}, bf16[4096,256]{1,0:T(8,128)(2,1)S(1)}, u32[]{:S(2)}, u32[]{:S(2)}) collective-permute-start(bf16[4096,256]{1,0:T(8,128)(2,1)} %get-tuple-element.11), channel_id=1, source_target_pairs={{0,1},{1,0},{2,3},{3,2},{4,5},{5,4},{6,7},{7,6},{8,9},{9,8},{10,11... | collective-permute-start | bytes 6291464 | tf_op jit(solution)/shard_map/ppermute | solution.py:187

commit v2 on v1

v2 whole, which is shorter than its diff:
```python
import jax
import jax.numpy as jnp
from jax import lax
from jax.experimental import pallas as pl
from jax.experimental.pallas import tpu as pltpu
from jax.sharding import PartitionSpec as P

BLK = 128
HD = 128
NBLK = 64
NDOC = 16
SIDE = 4
HALF = NBLK // 2
CHUNK = 4
REACH = 17
LIST = 24
ROWS_AT = 4 * LIST
COUNT_AT = 8 * LIST
META = 256
NEG = -1e30
SCALE = HD**-0.5
SCALE2 = SCALE * 1.4426950408889634
LANES = 2 * BLK

NT = (((1,), (1,)), ((), ()))
NN = (((1,), (0,)), ((), ()))
TN = (((0,), (0,)), ((), ()))
KEYS, VALS = slice(0, HD), slice(HD, 2 * HD)


def device_of(y, x, core):
    return (y % SIDE) * 2 * SIDE + (x % SIDE) * 2 + core


def along(axis_of_core):
    groups = []
    for core in range(2):
        for fixed in range(SIDE):
            if axis_of_core[core] == "y":
                groups.append([device_of(i, fixed, core) for i in range(SIDE)])
            else:
                groups.append([device_of(fixed, i, core) for i in range(SIDE)])
    return groups


FIRST = along("yx")
SECOND = along("xy")
SWAP = [(i, i ^ 1) for i in range(2 * SIDE * SIDE)]


def mm(a, b, dims):
    return lax.dot_general(a, b, dims, preferred_element_type=jnp.float32)


def stacked(ref, i):
    rows = pl.ds(i * BLK, BLK)
    return jnp.concatenate([ref[rows, :HD], ref[rows, HD:]], axis=0)


def unstack(ref, i, value):
    rows = pl.ds(i * BLK, BLK)
    ref[rows, :HD] = value[:BLK]
    ref[rows, HD:] = value[BLK:]


def place(meta, base, n):
    return pl.multiple_of(meta[ROWS_AT + base + n] * BLK, BLK)


def load(kv, meta, base, t, cols):
    return jnp.concatenate(
        [kv[pl.ds(place(meta, base, t * CHUNK + j), BLK), cols] for j in range(CHUNK)], axis=0
    )


def masked(s, meta, vec, i, base, t, sub):
    qstart, qpos = vec[2 * i : 2 * i + 1, :], vec[2 * i + 1 : 2 * i + 2, :]
    parts = []
    for j in range(CHUNK):
        first = meta[base + t * CHUNK + j] * BLK
        ok = (sub >= qstart - first) & (sub <= qpos - first)
        parts.append(jnp.where(ok, s[j * BLK : (j + 1) * BLK], NEG))
    return parts


def trips_of(meta, i, plane):
    return (meta[COUNT_AT + 2 * i + plane] + CHUNK - 1) // CHUNK


def iota_sub():
    return lax.broadcasted_iota(jnp.int32, (BLK, LANES), 0)


def chunk_at(t):
    return pl.ds(pl.multiple_of(t * CHUNK * BLK, CHUNK * BLK), CHUNK * BLK)


def tops(parts):
    best = jnp.maximum(jnp.maximum(parts[0], parts[1]), jnp.maximum(parts[2], parts[3]))
    return jnp.max(best, axis=0, keepdims=True)


def first_pass(order, lengths, q_ref, own_hbm, meta, vec, stat, part, kv, table, sem):
    copy = pltpu.make_async_copy(own_hbm, kv, sem)
    copy.start()
    me = lax.axis_index("ctx")
    core = me % 2

    def find(s, _):
        dev = s // 2
        y, x, c = dev // (2 * SIDE), (dev // 2) % SIDE, dev % 2
        slot = jnp.where(c == 0, x * SIDE + y, y * SIDE + x) * 2 + s % 2
        table[order[s]] = jnp.where(c == core, slot, slot + HALF)
        return 0

    lax.fori_loop(0, NBLK, find, 0, unroll=8)
    lane = lax.broadcasted_iota(jnp.int32, (1, LANES), 1) & (BLK - 1)
    for i in range(2):
        blk = order[2 * me + i]
        qpos = blk * BLK + lane
        end, low = jnp.int32(0), jnp.int32(0)
        qstart = jnp.zeros((1, LANES), jnp.int32)
        for d in range(NDOC):
            end = end + lengths[d]
            qstart = jnp.where(qpos >= end, end, qstart)
            low = jnp.where(blk * BLK >= end, end, low)
        vec[2 * i : 2 * i + 1, :] = qstart
        vec[2 * i + 1 : 2 * i + 2, :] = qpos
        low = low // BLK
        mine, others = jnp.int32(2 * i * LIST), jnp.int32((2 * i + 1) * LIST)
        for j in range(REACH):
            p = blk - j
            slot = table[jnp.maximum(p, 0)]
            away = slot >= HALF
            at = jnp.where(away, others, mine)
            meta[at] = p
            meta[ROWS_AT + at] = slot & (HALF - 1)
            step = jnp.where(p >= low, 1, 0)
            others = others + jnp.where(away, step, 0)
            mine = mine + jnp.where(away, 0, step)
        meta[COUNT_AT + 2 * i] = mine - 2 * i * LIST
        meta[COUNT_AT + 2 * i + 1] = others - (2 * i + 1) * LIST
        for j in range(CHUNK):
            for at in (mine, others):
                meta[at + j] = -1024
                meta[ROWS_AT + at + j] = 0
    copy.wait()
    sub = iota_sub()
    for i in range(2):
        qs = stacked(q_ref, i)
        base = 2 * i * LIST

        def step(t, carry):
            top, total, out = carry
            s = mm(load(kv, meta, base, t, KEYS), qs, NT)
            parts = masked(s, meta, vec, i, base, t, sub)
            new = jnp.maximum(top, tops(parts))
            shrink = jnp.exp2((top - new) * SCALE2)
            p = jnp.exp2((jnp.concatenate(parts, axis=0) - new) * SCALE2)
            total = total * shrink + jnp.sum(p, axis=0, keepdims=True)
            out = out * shrink + mm(load(kv, meta, base, t, VALS), p.astype(jnp.bfloat16), TN)
            return new, total, out

        top, total, out = lax.fori_loop(
            0,
            trips_of(meta, i, 0),
            step,
            (
                jnp.full((1, LANES), NEG, jnp.float32),
                jnp.zeros((1, LANES), jnp.float32),
                jnp.zeros((HD, LANES), jnp.float32),
            ),
        )
        stat[2 * i : 2 * i + 1, :] = top
        stat[2 * i + 1 : 2 * i + 2, :] = total
        part[i] = out


def add_to(ref, meta, base, t, dk, dv):
    for j in range(CHUNK):
        to = pl.ds(place(meta, base, t * CHUNK + j), BLK)
        rows = slice(j * BLK, (j + 1) * BLK)
        ref[to, KEYS] = (ref[to, KEYS].astype(jnp.float32) + dk[rows]).astype(jnp.bfloat16)
        ref[to, VALS] = (ref[to, VALS].astype(jnp.float32) + dv[rows]).astype(jnp.bfloat16)


def second_pass(meta, vec, stat, q_ref, g_ref, part, oth_hbm, o_ref, lse, dq_ref, dkv, kv, s_ref, p_ref, sem):
    copy = pltpu.make_async_copy(oth_hbm, kv, sem)
    copy.start()
    dkv[...] = jnp.zeros_like(dkv)
    sub = iota_sub()
    copy.wait()
    for i in range(2):
        qs, gs = stacked(q_ref, i), stacked(g_ref, i)
        base = (2 * i + 1) * LIST
        trips = trips_of(meta, i, 1)
        old_top, old_total = stat[2 * i : 2 * i + 1, :], stat[2 * i + 1 : 2 * i + 2, :]

        def scores(t, top):
            s = mm(load(kv, meta, base, t, KEYS), qs, NT)
            parts = masked(s, meta, vec, i, base, t, sub)
            s_ref[chunk_at(t), :] = jnp.concatenate(parts, axis=0)
            return jnp.maximum(top, tops(parts))

        top = lax.fori_loop(0, trips, scores, old_top)
        shrink = jnp.exp2((old_top - top) * SCALE2)

        def outputs(t, carry):
            total, out = carry
            p = jnp.exp2((s_ref[chunk_at(t), :] - top) * SCALE2)
            total = total + jnp.sum(p, axis=0, keepdims=True)
            p = p.astype(jnp.bfloat16)
            p_ref[chunk_at(t), :] = p
            return total, out + mm(load(kv, meta, base, t, VALS), p, TN)

        total, out = lax.fori_loop(0, trips, outputs, (old_total * shrink, part[i] * shrink))
        inv = 1.0 / total
        att = (out * inv).T.astype(jnp.bfloat16)
        unstack(o_ref, i, att)
        delta = jnp.sum((gs.astype(jnp.float32) * att.astype(jnp.float32)).T, axis=0, keepdims=True)
        lse[2 * i : 2 * i + 1, :] = top * SCALE2 + jnp.log2(total)
        lse[2 * i + 1 : 2 * i + 2, :] = delta
        scaled = inv * SCALE

        def grads(t, dq):
            p = p_ref[chunk_at(t), :].astype(jnp.float32)
            dp = mm(load(kv, meta, base, t, VALS), gs, NT)
            ds = ((p * scaled) * (dp - delta)).astype(jnp.bfloat16)
            dv = mm((p * inv).astype(jnp.bfloat16), gs, NN)
            dk = mm(ds, qs, NN)
            add_to(dkv, meta, base, t, dk, dv)
            return dq + mm(load(kv, meta, base, t, KEYS), ds, TN)

        dq_ref[i] = lax.fori_loop(0, trips, grads, jnp.zeros((HD, LANES), jnp.float32))


def third_pass(meta, vec, lse, q_ref, g_ref, dq_in, own_hbm, dq_ref, dkv, kv, sem):
    copy = pltpu.make_async_copy(own_hbm, kv, sem)
    copy.start()
    dkv[...] = jnp.zeros_like(dkv)
    sub = iota_sub()
    copy.wait()
    for i in range(2):
        qs, gs = stacked(q_ref, i), stacked(g_ref, i)
        base = 2 * i * LIST
        logsum, delta = lse[2 * i : 2 * i + 1, :], lse[2 * i + 1 : 2 * i + 2, :]

        def grads(t, dq):
            keys = load(kv, meta, base, t, KEYS)
            parts = masked(mm(keys, qs, NT), meta, vec, i, base, t, sub)
            p = jnp.exp2(jnp.concatenate(parts, axis=0) * SCALE2 - logsum)
            dp = mm(load(kv, meta, base, t, VALS), gs, NT)
            ds = ((p * SCALE) * (dp - delta)).astype(jnp.bfloat16)
            dv = mm(p.astype(jnp.bfloat16), gs, NN)
            dk = mm(ds, qs, NN)
            add_to(dkv, meta, base, t, dk, dv)
            return dq + mm(keys, ds, TN)

        dq = lax.fori_loop(0, trips_of(meta, i, 0), grads, dq_in[i])
        unstack(dq_ref, i, dq.T.astype(jnp.bfloat16))


SMEM = pl.BlockSpec(memory_space=pltpu.SMEM)
VMEM = pl.BlockSpec(memory_space=pltpu.VMEM)
ANY = pl.BlockSpec(memory_space=pl.ANY)


def shape(*dims, dtype=jnp.bfloat16):
    return jax.ShapeDtypeStruct(dims, dtype)


def kernel(body, name, ins, outs, out_specs, scratch, flops, size):
    return pl.pallas_call(
        body,
        out_shape=outs,
        in_specs=ins,
        out_specs=out_specs,
        scratch_shapes=scratch,
        compiler_params=pltpu.CompilerParams(vmem_limit_bytes=48 * 1024 * 1024),
        cost_estimate=pl.CostEstimate(flops=flops, bytes_accessed=size, transcendentals=0),
        name=name,
    )


def per_device(queries, key_rows, value_rows, grad_output, doc_lengths, block_order):
    tokens = queries.shape[0]
    f32, i32, bf16 = jnp.float32, jnp.int32, jnp.bfloat16
    plane = HALF * BLK
    buffer = pltpu.VMEM((plane, 2 * HD), bf16)
    sem = pltpu.SemaphoreType.DMA
    kv = jnp.concatenate([key_rows, value_rows], axis=1)
    line = lax.all_gather(kv, "ctx", axis=0, tiled=True, axis_index_groups=FIRST)
    spread = jnp.broadcast_to(line[None], (SIDE,) + line.shape)
    own = lax.all_to_all(spread, "ctx", 0, 0, tiled=True, axis_index_groups=SECOND)
    own = own.reshape(plane, 2 * HD)
    oth = lax.ppermute(own, "ctx", SWAP)
    wide = shape(2, HD, LANES, dtype=f32)
    small = shape(4, LANES, dtype=f32)
    meta, vec, stat, part = kernel(
        first_pass,
        "forward_own",
        [SMEM, SMEM, VMEM, ANY],
        (shape(META, dtype=i32), shape(4, LANES, dtype=i32), small, wide),
        (SMEM, VMEM, VMEM, VMEM),
        [buffer, pltpu.SMEM((NBLK,), i32), sem],
        2 * 10**9,
        4 * 10**6,
    )(block_order, doc_lengths, queries, own)
    attention, lse, dq, dkv_oth = kernel(
        second_pass,
        "other_plane",
        [SMEM, VMEM, VMEM, VMEM, VMEM, VMEM, ANY],
        (shape(tokens, 2 * HD), small, wide, shape(plane, 2 * HD)),
        (VMEM,) * 4,
        [buffer, pltpu.VMEM((LIST * BLK, LANES), f32), pltpu.VMEM((LIST * BLK, LANES), bf16), sem],
        4 * 10**9,
        6 * 10**6,
    )(meta, vec, stat, queries, grad_output, part, oth)
    back = lax.ppermute(dkv_oth, "ctx", SWAP)
    grad_queries, dkv_own = kernel(
        third_pass,
        "backward_own",
        [SMEM, VMEM, VMEM, VMEM, VMEM, VMEM, ANY],
        (shape(tokens, 2 * HD), shape(plane, 2 * HD)),
        (VMEM,) * 2,
        [buffer, sem],
        3 * 10**9,
        6 * 10**6,
    )(meta, vec, lse, queries, grad_output, dq, own)
    part = (dkv_own.astype(f32) + back.astype(f32)).astype(bf16)
    part = part.reshape(SIDE, SIDE * tokens, 2 * HD)
    part = lax.all_to_all(part, "ctx", 0, 0, tiled=True, axis_index_groups=SECOND)
    part = jnp.sum(part.astype(f32), axis=0).astype(bf16).reshape(SIDE, tokens, 2 * HD)
    part = lax.all_to_all(part, "ctx", 0, 0, tiled=True, axis_index_groups=FIRST)
    part = jnp.sum(part.astype(f32), axis=0).astype(bf16)
    return attention, grad_queries, part[:, :HD], part[:, HD:]


def solution(mesh):
    rows = P(("dp", "ctx"), None)
    return jax.shard_map(
        per_device,
        mesh=mesh,
        in_specs=(rows, rows, rows, rows, P("dp"), P("dp")),
        out_specs=(rows, rows, rows, rows),
        check_vma=False,
    )
```

time: 91.8 us -> 85.5 us (0.931); the launches traced: 91.5 us -> 83.8 us
  waiting for transfers between devices: 8.15 us -> 1.01 us
  local copies, waits for them, and re-layouts: 2.13 us -> 0.82 us
  Pallas kernels: 9.81 us -> 10.9 us
    ppermute x1, waiting for transfers between devices: 4.16 us -> 0.13 us  [per_device(): oth = lax.ppermute(own, 'ctx', SWAP)]
    ppermute x1, waiting for transfers between devices: 4 us -> 0.88 us  [per_device(): back = lax.ppermute(dkv_oth, 'ctx', SWAP)]
    all_to_all x1, blocking collectives: 13.4 us -> 12 us  [per_device(): lax.all_to_all(part, 'ctx', 0, 0, tiled=True, axis_index_groups=FIRST)]
    unnamed x12 -> x8, local copies, waits for them, and re-layouts: 1.34 us -> 0.02 us
    all_to_all x1, blocking collectives: 19 us -> 20.1 us  [per_device(): lax.all_to_all(part, 'ctx', 0, 0, tiled=True, axis_index_groups=SECOND)]
    pallas_call x1 -> x3, Pallas kernels: 9.81 us -> 10.9 us  [the longest x1 4.01 us: per_device(): kernel(second_pass, 'other_plane', [SMEM, VMEM, VMEM, VMEM, VMEM, VMEM, A...]
  transfers between devices with their start and end apart: 2 -> 2, of which waited for: 2 -> 2; matrix products, arithmetic and copies ran while one was open for 0% -> 0% of each run, Pallas kernels for 0% -> 8%
where the time goes in v2:
time: 85.5 us; the launch traced here: 83.8 us
  blocking collectives  66.1 us (77%)
  Pallas kernels  10.9 us (13%)
  other arithmetic  2.21 us (3%)
  starting transfers between devices  2.03 us (2%)
  waiting for transfers between devices  1.01 us (1%)
    all_to_all x1, blocking collectives, per_device(): lax.all_to_all(spread, 'ctx', 0, 0, tiled=True, axis_index_groups=SECOND)  20.7 us
    all_to_all x1, blocking collectives, per_device(): lax.all_to_all(part, 'ctx', 0, 0, tiled=True, axis_index_groups=SECOND)  20.1 us
    all_gather x1, blocking collectives, per_device(): lax.all_gather(kv, 'ctx', axis=0, tiled=True, axis_index_groups=FIRST)  13.3 us
    all_to_all x1, blocking collectives, per_device(): lax.all_to_all(part, 'ctx', 0, 0, tiled=True, axis_index_groups=FIRST)  12 us
    pallas_call x1, Pallas kernels, per_device(): kernel(second_pass, 'other_plane', [SMEM, VMEM, VMEM, VMEM, VMEM, VMEM, A...  4.01 us
    pallas_call x1, Pallas kernels, per_device(): kernel(first_pass, 'forward_own', [SMEM, SMEM, VMEM, ANY], (shape(META, d...  3.99 us
    pallas_call x1, Pallas kernels, per_device(): kernel(third_pass, 'backward_own', [SMEM, VMEM, VMEM, VMEM, VMEM, VMEM, A...  2.9 us
    ppermute x1, starting transfers between devices, per_device(): back = lax.ppermute(dkv_oth, 'ctx', SWAP)  2.03 us
  transfers between devices with their start and end apart: 2, of which 2 were waited for; matrix products, arithmetic and copies ran while one was open for 0% of the time, Pallas kernels for 8%

profile of v2, /device:TPU:160, one launch (start us, length us, event | category | flops | bytes accessed | tf_op | source)
XLA Modules:
  0.0 83.8 jit_solution(7510072198886888308)
XLA Ops:
  0.6 0.9 %pad_maximum_fusion = bf16[256,256]{1,0:T(8,128)(2,1)S(1)} fusion(bf16[256,128]{1,0:T(8,128)(2,1)} %param.8, bf16[256,128]{1,0:T(8,128)(2,1)} %param.7), kind=kLoop, calls=%fused_computation.1 | loop fusion | flops 262144 | bytes 262144 | tf_op jit(solution)/shard_map/concatenate | solution.py:291
  1.5 13.3 %all_gather.3 = bf16[1024,256]{1,0:T(8,128)(2,1)S(1)} all-gather(bf16[256,256]{1,0:T(8,128)(2,1)S(1)} %pad_maximum_fusion), channel_id=1, replica_groups={{0,8,16,24},{2,10,18,26},{4,12,20,28},{6,14,22,30},{1,3,5,7},{9,11,13,1..., dimensions={0}, use_global_device_ids=true | all-gather | bytes 655360 | tf_op jit(solution)/shard_map/all_gather | solution.py:292
  14.8 0.1 broadcast_in_dim.2
  15.0 0.0 copy-start
  15.0 0.0 copy-start.2
  15.0 0.0 copy-start.3
  15.0 20.7 %all_to_all.15 = bf16[4,1024,256]{2,1,0:T(8,128)(2,1)S(1)} all-to-all(bf16[4,1024,256]{2,1,0:T(8,128)(2,1)S(1)} %broadcast_in_dim.2), channel_id=1, replica_groups={{0,2,4,6},{8,10,12,14},{16,18,20,22},{24,26,28,30},{1,9,17,25},{3,11,19..., dimensions={0} | all-to-all | bytes 4194304 | tf_op jit(solution)/shard_map/all_to_all | solution.py:294
  35.7 0.0 copy-start.1
  35.7 0.0 collective-permute-start
  35.7 0.0 copy-done
  35.8 0.0 copy-done.2
  35.8 0.0 copy-done.3
  35.8 4.0 %forward_own.1 = (s32[256]{0:T(256)S(1)}, s32[4,256]{1,0:T(4,128)S(1)}, f32[4,256]{1,0:T(4,128)S(1)}, f32[2,128,256]{2,1,0:T(8,128)S(1)}) custom-call(s32[64]{0:T(128)S(1)} %copy-done.2, s32[16]{0:T(128)S(1)} %copy-done.3, bf16[256,256]{1,0:T(8,128)(2,1)S(1)} %copy-done, bf16[4096,256]{1,0:T(8,128)(2,1)S(1)} %bitcast.4), custom_call_target="tpu_custom_call" | custom-call | flops 2000000000 | bytes 4000000 | tf_op jit(solution)/shard_map/forward_own/pallas_call | solution.py:299
  39.8 0.1 collective-permute-done.oth_hbm
  39.9 0.0 copy-done.1
  39.9 4.0 %other_plane.1 = (bf16[256,256]{1,0:T(8,128)(2,1)}, f32[4,256]{1,0:T(4,128)S(1)}, f32[2,128,256]{2,1,0:T(8,128)S(1)}, bf16[4096,256]{1,0:T(8,128)(2,1)S(1)}) custom-call(s32[256]{0:T(256)S(1)} %get-tuple-element.14.meta, s32[4,256]{1,0:T(4,128)S(1)} %get-tuple-element.15.vec, f32[4,256]{1,0:T(4,128)S(1)} %get-tuple-element.16.stat, ...), custom_call_target="tpu_custom_call" | custom-call | flops 4000000000 | bytes 6000000 | tf_op jit(solution)/shard_map/other_plane/pallas_call | solution.py:309
  43.9 2.0 %collective-permute-start.1 = (bf16[4096,256]{1,0:T(8,128)(2,1)S(1)}, bf16[4096,256]{1,0:T(8,128)(2,1)S(1)}, u32[]{:S(2)}, u32[]{:S(2)}) collective-permute-start(bf16[4096,256]{1,0:T(8,128)(2,1)S(1)} %get-tuple-element.23), channel_id=1, source_target_pairs={{0,1},{1,0},{2,3},{3,2},{4,5},{5,4},{6,7},{7,6},{8,9},{9,8},{10,11... | collective-permute-start | bytes 6291464 | tf_op jit(solution)/shard_map/ppermute | solution.py:319
  46.0 2.9 %backward_own.1 = (bf16[256,256]{1,0:T(8,128)(2,1)}, bf16[4096,256]{1,0:T(8,128)(2,1)S(1)}) custom-call(s32[256]{0:T(256)S(1)} %get-tuple-element.14.meta, s32[4,256]{1,0:T(4,128)S(1)} %get-tuple-element.15.vec, f32[4,256]{1,0:T(4,128)S(1)} %get-tuple-element.19.lse, bf16[256,256]{1,0:T(8,128)(2,1)S(1)} %copy-done, bf16[256,256]{1,0:T(8,128)(2,1)S(1)} %copy-done.1, ...), custom_call_target="tpu_custom_call" | custom-call | flops 3000000000 | bytes 6000000 | tf_op jit(solution)/shard_map/backward_own/pallas_call | solution.py:320
  48.9 0.9 %collective-permute-done.1 = bf16[4096,256]{1,0:T(8,128)(2,1)S(1)} collective-permute-done((bf16[4096,256]{1,0:T(8,128)(2,1)S(1)}, bf16[4096,256]{1,0:T(8,128)(2,1)S(1)}, u32[]{:S(2)}, u32[]{:S(2)}) %collective-permute-start.1) | collective-permute-done | bytes 2097184 | tf_op jit(solution)/shard_map/ppermute | solution.py:319
  49.7 0.6 add_convert_fusion
  50.3 20.1 %all_to_all.16 = bf16[4,1024,256]{2,1,0:T(8,128)(2,1)S(1)} all-to-all(bf16[4,1024,256]{2,1,0:T(8,128)(2,1)S(1)} %bitcast.6), channel_id=1, replica_groups={{0,2,4,6},{8,10,12,14},{16,18,20,22},{24,26,28,30},{1,9,17,25},{3,11,19..., dimensions={0} | all-to-all | bytes 4194304 | tf_op jit(solution)/shard_map/all_to_all | solution.py:332
  70.4 0.6 reduce_sum.24
  71.1 12.0 %all_to_all.17 = bf16[4,256,256]{2,1,0:T(8,128)(2,1)S(1)} all-to-all(bf16[4,256,256]{2,1,0:T(8,128)(2,1)S(1)} %bitcast.7), channel_id=1, replica_groups={{0,8,16,24},{2,10,18,26},{4,12,20,28},{6,14,22,30},{1,3,5,7},{9,11,13,1..., dimensions={0} | all-to-all | bytes 1048576 | tf_op jit(solution)/shard_map/all_to_all | solution.py:334
  83.1 0.1 reduce_sum.25
  83.2 0.7 fusion
Async XLA Ops:
  15.0 20.8 %copy-start = (bf16[256,256]{1,0:T(8,128)(2,1)S(1)}, bf16[256,256]{1,0:T(8,128)(2,1)}, u32[]{:S(2)}) copy-start(bf16[256,256]{1,0:T(8,128)(2,1)} %q_ref.5) | copy-start | bytes 393220
  15.0 20.8 %copy-start.2 = (s32[64]{0:T(128)S(1)}, s32[64]{0:T(128)}, u32[]{:S(2)}) copy-start(s32[64]{0:T(128)} %order.1) | copy-start | bytes 772
  15.0 20.8 %copy-start.3 = (s32[16]{0:T(128)S(1)}, s32[16]{0:T(128)}, u32[]{:S(2)}) copy-start(s32[16]{0:T(128)} %lengths.1) | copy-start | bytes 196
  35.7 4.2 %copy-start.1 = (bf16[256,256]{1,0:T(8,128)(2,1)S(1)}, bf16[256,256]{1,0:T(8,128)(2,1)}, u32[]{:S(2)}) copy-start(bf16[256,256]{1,0:T(8,128)(2,1)} %g_ref.3) | copy-start | bytes 393220
  35.7 4.2 %collective-permute-start = (bf16[4096,256]{1,0:T(8,128)(2,1)S(1)}, bf16[4096,256]{1,0:T(8,128)(2,1)S(1)}, u32[]{:S(2)}, u32[]{:S(2)}) collective-permute-start(bf16[4096,256]{1,0:T(8,128)(2,1)S(1)} %bitcast.3), channel_id=1, source_target_pairs={{0,1},{1,0},{2,3},{3,2},{4,5},{5,4},{6,7},{7,6},{8,9},{9,8},{10,11... | collective-permute-start | bytes 6291464 | tf_op jit(solution)/shard_map/ppermute | solution.py:296
  43.9 5.8 %collective-permute-start.1 = (bf16[4096,256]{1,0:T(8,128)(2,1)S(1)}, bf16[4096,256]{1,0:T(8,128)(2,1)S(1)}, u32[]{:S(2)}, u32[]{:S(2)}) collective-permute-start(bf16[4096,256]{1,0:T(8,128)(2,1)S(1)} %get-tuple-element.23), channel_id=1, source_target_pairs={{0,1},{1,0},{2,3},{3,2},{4,5},{5,4},{6,7},{7,6},{8,9},{9,8},{10,11... | collective-permute-start | bytes 6291464 | tf_op jit(solution)/shard_map/ppermute | solution.py:319

commit v3 on v2

v3 whole, which is shorter than its diff:
```python
import jax
import jax.numpy as jnp
from jax import lax
from jax.experimental import pallas as pl
from jax.experimental.pallas import tpu as pltpu
from jax.sharding import PartitionSpec as P

BLK = 128
HD = 128
NBLK = 64
NDOC = 16
SIDE = 4
HALF = NBLK // 2
CHUNK = 4
REACH = 17
LIST = 24
ROWS_AT = 4 * LIST
COUNT_AT = 8 * LIST
META = 256
NEG = -1e30
SCALE = HD**-0.5
SCALE2 = SCALE * 1.4426950408889634
LANES = 2 * BLK

NT = (((1,), (1,)), ((), ()))
NN = (((1,), (0,)), ((), ()))
TN = (((0,), (0,)), ((), ()))
KEYS, VALS = slice(0, HD), slice(HD, 2 * HD)


def device_of(y, x, core):
    return (y % SIDE) * 2 * SIDE + (x % SIDE) * 2 + core


def along(axis_of_core):
    groups = []
    for core in range(2):
        for fixed in range(SIDE):
            if axis_of_core[core] == "y":
                groups.append([device_of(i, fixed, core) for i in range(SIDE)])
            else:
                groups.append([device_of(fixed, i, core) for i in range(SIDE)])
    return groups


FIRST = along("yx")
SECOND = along("xy")
SWAP = [(i, i ^ 1) for i in range(2 * SIDE * SIDE)]


def mm(a, b, dims):
    return lax.dot_general(a, b, dims, preferred_element_type=jnp.float32)


def stacked(ref, i):
    rows = pl.ds(i * BLK, BLK)
    return jnp.concatenate([ref[rows, :HD], ref[rows, HD:]], axis=0)


def unstack(ref, i, value):
    rows = pl.ds(i * BLK, BLK)
    ref[rows, :HD] = value[:BLK]
    ref[rows, HD:] = value[BLK:]


def place(meta, base, n):
    return pl.multiple_of(meta[ROWS_AT + base + n] * BLK, BLK)


def load(kv, meta, base, t, cols):
    return jnp.concatenate(
        [kv[pl.ds(place(meta, base, t * CHUNK + j), BLK), cols] for j in range(CHUNK)], axis=0
    )


def chunk_at(t):
    return pl.ds(pl.multiple_of(t * CHUNK * BLK, CHUNK * BLK), CHUNK * BLK)


def scores_of(keys, qs, meta, vec, i, base, t):
    s = mm(keys, qs, NT)
    sub = lax.broadcasted_iota(jnp.int32, (BLK, LANES), 0)
    qstart, qpos = vec[2 * i : 2 * i + 1, :], vec[2 * i + 1 : 2 * i + 2, :]
    parts = []
    for j in range(CHUNK):
        first = meta[base + t * CHUNK + j] * BLK
        ok = (sub >= qstart - first) & (sub <= qpos - first)
        parts.append(jnp.where(ok, s[j * BLK : (j + 1) * BLK], NEG))
    return jnp.concatenate(parts, axis=0)


def trips_of(meta, plane):
    most = jnp.maximum(meta[COUNT_AT + plane], meta[COUNT_AT + 2 + plane])
    return (most + CHUNK - 1) // CHUNK


def tops(s):
    return jnp.max(s, axis=0, keepdims=True)


def first_pass(order, lengths, q_ref, own_hbm, meta, vec, stat, part, kv, table, sem):
    copy = fetch_all(own_hbm, kv, sem)
    me = lax.axis_index("ctx")
    core = me & 1
    for s in range(NBLK):
        dev = s // 2
        y, x, c = dev // (2 * SIDE), (dev // 2) % SIDE, dev % 2
        slot = (y * SIDE + x if c else x * SIDE + y) * 2 + s % 2
        table[order[s]] = slot + (HALF * (1 - core) if c else HALF * core)
    lane = lax.broadcasted_iota(jnp.int32, (1, LANES), 1) & (BLK - 1)
    for i in range(2):
        blk = order[2 * me + i]
        qpos = blk * BLK + lane
        end, low = jnp.int32(0), jnp.int32(0)
        qstart = jnp.zeros((1, LANES), jnp.int32)
        for d in range(NDOC):
            end = end + lengths[d]
            qstart = jnp.where(qpos >= end, end, qstart)
            low = jnp.where(blk * BLK >= end, end, low)
        vec[2 * i : 2 * i + 1, :] = qstart
        vec[2 * i + 1 : 2 * i + 2, :] = qpos
        low = low >> 7
        for j in range(2 * LIST):
            meta[2 * i * LIST + j] = -1024
            meta[ROWS_AT + 2 * i * LIST + j] = 0
        mine, others = jnp.int32(2 * i * LIST), jnp.int32((2 * i + 1) * LIST)
        for j in range(REACH):
            p = blk - j
            slot = table[jnp.maximum(p, 0)]
            away = slot >= HALF
            at = jnp.where(away, others, mine)
            meta[at] = p
            meta[ROWS_AT + at] = slot & (HALF - 1)
            step = jnp.where(p >= low, 1, 0)
            others = others + jnp.where(away, step, 0)
            mine = mine + jnp.where(away, 0, step)
        meta[COUNT_AT + 2 * i] = mine - 2 * i * LIST
        meta[COUNT_AT + 2 * i + 1] = others - (2 * i + 1) * LIST
        meta[mine] = -1024
        meta[others] = -1024
    copy.wait()
    qs = [stacked(q_ref, i) for i in range(2)]

    def step(t, carry):
        after = []
        for i in range(2):
            top, total, out = carry[i]
            base = 2 * i * LIST
            s = scores_of(load(kv, meta, base, t, KEYS), qs[i], meta, vec, i, base, t)
            new = jnp.maximum(top, tops(s))
            shrink = jnp.exp2((top - new) * SCALE2)
            p = jnp.exp2((s - new) * SCALE2)
            total = total * shrink + jnp.sum(p, axis=0, keepdims=True)
            out = out * shrink + mm(load(kv, meta, base, t, VALS), p.astype(jnp.bfloat16), TN)
            after.append((new, total, out))
        return tuple(after)

    empty = (
        jnp.full((1, LANES), NEG, jnp.float32),
        jnp.zeros((1, LANES), jnp.float32),
        jnp.zeros((HD, LANES), jnp.float32),
    )
    for i, (top, total, out) in enumerate(lax.fori_loop(0, trips_of(meta, 0), step, (empty, empty))):
        stat[2 * i : 2 * i + 1, :] = top
        stat[2 * i + 1 : 2 * i + 2, :] = total
        part[i] = out


def fetch_all(hbm, kv, sem):
    copy = pltpu.make_async_copy(hbm, kv, sem)
    copy.start()
    return copy


def put(ref, meta, base, t, dk, dv):
    for j in range(CHUNK):
        to = pl.ds(place(meta, base, t * CHUNK + j), BLK)
        rows = slice(j * BLK, (j + 1) * BLK)
        ref[to, KEYS] = (ref[to, KEYS].astype(jnp.float32) + dk[rows]).astype(jnp.bfloat16)
        ref[to, VALS] = (ref[to, VALS].astype(jnp.float32) + dv[rows]).astype(jnp.bfloat16)


def second_pass(meta, vec, stat, q_ref, g_ref, part, oth_hbm, o_ref, lse, dq_ref, dkv, kv, s_ref, p_ref, sem):
    copy = fetch_all(oth_hbm, kv, sem)
    dkv[...] = jnp.zeros_like(dkv)
    copy.wait()
    both = range(2)
    qs, gs = [stacked(q_ref, i) for i in both], [stacked(g_ref, i) for i in both]
    base = [(2 * i + 1) * LIST for i in both]
    trips = trips_of(meta, 1)
    old_top = [stat[2 * i : 2 * i + 1, :] for i in both]

    def scores(t, tops_so_far):
        after = []
        for i in both:
            s = scores_of(load(kv, meta, base[i], t, KEYS), qs[i], meta, vec, i, base[i], t)
            s_ref[i, chunk_at(t), :] = s
            after.append(jnp.maximum(tops_so_far[i], tops(s)))
        return tuple(after)

    top = lax.fori_loop(0, trips, scores, tuple(old_top))

    def outputs(t, carry):
        after = []
        for i in both:
            total, out = carry[i]
            p = jnp.exp2((s_ref[i, chunk_at(t), :] - top[i]) * SCALE2)
            total = total + jnp.sum(p, axis=0, keepdims=True)
            p = p.astype(jnp.bfloat16)
            p_ref[i, chunk_at(t), :] = p
            after.append((total, out + mm(load(kv, meta, base[i], t, VALS), p, TN)))
        return tuple(after)

    start = []
    for i in both:
        shrink = jnp.exp2((old_top[i] - top[i]) * SCALE2)
        start.append((stat[2 * i + 1 : 2 * i + 2, :] * shrink, part[i] * shrink))
    done = lax.fori_loop(0, trips, outputs, tuple(start))
    scaled, delta, over = [], [], []
    for i in both:
        total, out = done[i]
        inv = 1.0 / total
        att = (out * inv).T.astype(jnp.bfloat16)
        unstack(o_ref, i, att)
        wide = gs[i].astype(jnp.float32)
        delta.append(jnp.sum((wide * att.astype(jnp.float32)).T, axis=0, keepdims=True))
        lse[2 * i : 2 * i + 1, :] = top[i] * SCALE2 + jnp.log2(total)
        lse[2 * i + 1 : 2 * i + 2, :] = delta[i]
        scaled.append(inv * SCALE)
        over.append((wide * jnp.broadcast_to(inv, (HD, LANES)).T).astype(jnp.bfloat16))

    def grads(t, dq):
        after = []
        for i in both:
            p = p_ref[i, chunk_at(t), :]
            dp = mm(load(kv, meta, base[i], t, VALS), gs[i], NT)
            ds = ((p.astype(jnp.float32) * scaled[i]) * (dp - delta[i])).astype(jnp.bfloat16)
            put(dkv, meta, base[i], t, mm(ds, qs[i], NN), mm(p, over[i], NN))
            after.append(dq[i] + mm(load(kv, meta, base[i], t, KEYS), ds, TN))
        return tuple(after)

    zero = jnp.zeros((HD, LANES), jnp.float32)
    dq_ref[0], dq_ref[1] = lax.fori_loop(0, trips, grads, (zero, zero))


def third_pass(meta, vec, lse, q_ref, g_ref, dq_in, own_hbm, dq_ref, dkv, kv, sem):
    copy = fetch_all(own_hbm, kv, sem)
    dkv[...] = jnp.zeros_like(dkv)
    copy.wait()
    both = range(2)
    qs, gs = [stacked(q_ref, i) for i in both], [stacked(g_ref, i) for i in both]

    def grads(t, dq):
        after = []
        for i in both:
            base = 2 * i * LIST
            keys = load(kv, meta, base, t, KEYS)
            s = scores_of(keys, qs[i], meta, vec, i, base, t)
            p = jnp.exp2(s * SCALE2 - lse[2 * i : 2 * i + 1, :])
            dp = mm(load(kv, meta, base, t, VALS), gs[i], NT)
            ds = ((p * SCALE) * (dp - lse[2 * i + 1 : 2 * i + 2, :])).astype(jnp.bfloat16)
            put(dkv, meta, base, t, mm(ds, qs[i], NN), mm(p.astype(jnp.bfloat16), gs[i], NN))
            after.append(dq[i] + mm(keys, ds, TN))
        return tuple(after)

    for i, dq in enumerate(lax.fori_loop(0, trips_of(meta, 0), grads, (dq_in[0], dq_in[1]))):
        unstack(dq_ref, i, dq.T.astype(jnp.bfloat16))


SMEM = pl.BlockSpec(memory_space=pltpu.SMEM)
VMEM = pl.BlockSpec(memory_space=pltpu.VMEM)
ANY = pl.BlockSpec(memory_space=pl.ANY)


def shape(*dims, dtype=jnp.bfloat16):
    return jax.ShapeDtypeStruct(dims, dtype)


def kernel(body, name, ins, outs, out_specs, scratch, flops, size):
    return pl.pallas_call(
        body,
        out_shape=outs,
        in_specs=ins,
        out_specs=out_specs,
        scratch_shapes=scratch,
        compiler_params=pltpu.CompilerParams(vmem_limit_bytes=48 * 1024 * 1024),
        cost_estimate=pl.CostEstimate(flops=flops, bytes_accessed=size, transcendentals=0),
        name=name,
    )


def per_device(queries, key_rows, value_rows, grad_output, doc_lengths, block_order):
    tokens = queries.shape[0]
    f32, i32, bf16 = jnp.float32, jnp.int32, jnp.bfloat16
    plane = HALF * BLK
    padded = pltpu.VMEM((plane, 2 * HD), bf16)
    scores = pltpu.VMEM((2, LIST * BLK, LANES), f32)
    sem = pltpu.SemaphoreType.DMA
    kv = jnp.concatenate([key_rows, value_rows], axis=1)
    line = lax.all_gather(kv, "ctx", axis=0, tiled=True, axis_index_groups=FIRST)
    spread = jnp.broadcast_to(line[None], (SIDE,) + line.shape)
    own = lax.all_to_all(spread, "ctx", 0, 0, tiled=True, axis_index_groups=SECOND)
    own = own.reshape(plane, 2 * HD)
    oth = lax.ppermute(own, "ctx", SWAP)
    wide = shape(2, HD, LANES, dtype=f32)
    small = shape(4, LANES, dtype=f32)
    meta, vec, stat, part = kernel(
        first_pass,
        "forward_own",
        [SMEM, SMEM, VMEM, ANY],
        (shape(META, dtype=i32), shape(4, LANES, dtype=i32), small, wide),
        (SMEM, VMEM, VMEM, VMEM),
        [padded, pltpu.SMEM((NBLK,), i32), sem],
        2 * 10**9,
        4 * 10**6,
    )(block_order, doc_lengths, queries, own)
    attention, lse, dq, dkv_oth = kernel(
        second_pass,
        "other_plane",
        [SMEM, VMEM, VMEM, VMEM, VMEM, VMEM, ANY],
        (shape(tokens, 2 * HD), small, wide, shape(plane, 2 * HD)),
        (VMEM,) * 4,
        [padded, scores, pltpu.VMEM((2, LIST * BLK, LANES), bf16), sem],
        4 * 10**9,
        6 * 10**6,
    )(meta, vec, stat, queries, grad_output, part, oth)
    back = lax.ppermute(dkv_oth, "ctx", SWAP)
    grad_queries, dkv_own = kernel(
        third_pass,
        "backward_own",
        [SMEM, VMEM, VMEM, VMEM, VMEM, VMEM, ANY],
        (shape(tokens, 2 * HD), shape(plane, 2 * HD)),
        (VMEM,) * 2,
        [padded, sem],
        3 * 10**9,
        6 * 10**6,
    )(meta, vec, lse, queries, grad_output, dq, own)
    part = (dkv_own.astype(f32) + back.astype(f32)).astype(bf16)
    part = part.reshape(SIDE, SIDE * tokens, 2 * HD)
    part = lax.all_to_all(part, "ctx", 0, 0, tiled=True, axis_index_groups=SECOND)
    part = jnp.sum(part.astype(f32), axis=0).astype(bf16).reshape(SIDE, tokens, 2 * HD)
    part = lax.all_to_all(part, "ctx", 0, 0, tiled=True, axis_index_groups=FIRST)
    part = jnp.sum(part.astype(f32), axis=0).astype(bf16)
    return attention, grad_queries, part[:, :HD], part[:, HD:]


def solution(mesh):
    rows = P(("dp", "ctx"), None)
    return jax.shard_map(
        per_device,
        mesh=mesh,
        in_specs=(rows, rows, rows, rows, P("dp"), P("dp")),
        out_specs=(rows, rows, rows, rows),
        check_vma=False,
    )
```

time: 85.5 us -> 84.8 us (level)
  the two profiles are of different devices: /device:TPU:160 before, /device:TPU:128 now
where the time goes in v3:
time: 84.8 us; the launch traced here: 83.5 us
  blocking collectives  64.5 us (76%)
  Pallas kernels  11.1 us (13%)
  starting transfers between devices  3.82 us (5%)
  other arithmetic  2.21 us (3%)
    all_to_all x1, blocking collectives, per_device(): lax.all_to_all(spread, 'ctx', 0, 0, tiled=True, axis_index_groups=SECOND)  20.7 us
    all_to_all x1, blocking collectives, per_device(): lax.all_to_all(part, 'ctx', 0, 0, tiled=True, axis_index_groups=SECOND)  19 us
    all_gather x1, blocking collectives, per_device(): lax.all_gather(kv, 'ctx', axis=0, tiled=True, axis_index_groups=FIRST)  13.3 us
    all_to_all x1, blocking collectives, per_device(): lax.all_to_all(part, 'ctx', 0, 0, tiled=True, axis_index_groups=FIRST)  11.5 us
    pallas_call x1, Pallas kernels, per_device(): kernel(first_pass, 'forward_own', [SMEM, SMEM, VMEM, ANY], (shape(META, d...  4.01 us
    ppermute x1, starting transfers between devices, per_device(): back = lax.ppermute(dkv_oth, 'ctx', SWAP)  3.81 us
    pallas_call x1, Pallas kernels, per_device(): kernel(third_pass, 'backward_own', [SMEM, VMEM, VMEM, VMEM, VMEM, VMEM, A...  3.61 us
    pallas_call x1, Pallas kernels, per_device(): kernel(second_pass, 'other_plane', [SMEM, VMEM, VMEM, VMEM, VMEM, VMEM, A...  3.52 us
  transfers between devices with their start and end apart: 2, of which 2 were waited for; matrix products, arithmetic and copies ran while one was open for 0% of the time, Pallas kernels for 9%

profile of v3, /device:TPU:128, one launch (start us, length us, event | category | flops | bytes accessed | tf_op | source)
XLA Modules:
  0.0 83.5 jit_solution(12605073872563299642)
XLA Ops:
  0.6 0.9 %pad_maximum_fusion = bf16[256,256]{1,0:T(8,128)(2,1)S(1)} fusion(bf16[256,128]{1,0:T(8,128)(2,1)} %param.8, bf16[256,128]{1,0:T(8,128)(2,1)} %param.7), kind=kLoop, calls=%fused_computation.1 | loop fusion | flops 262144 | bytes 262144 | tf_op jit(solution)/shard_map/concatenate | solution.py:299
  1.5 13.3 %all_gather.3 = bf16[1024,256]{1,0:T(8,128)(2,1)S(1)} all-gather(bf16[256,256]{1,0:T(8,128)(2,1)S(1)} %pad_maximum_fusion), channel_id=1, replica_groups={{0,8,16,24},{2,10,18,26},{4,12,20,28},{6,14,22,30},{1,3,5,7},{9,11,13,1..., dimensions={0}, use_global_device_ids=true | all-gather | bytes 655360 | tf_op jit(solution)/shard_map/all_gather | solution.py:300
  14.8 0.1 broadcast_in_dim.2
  15.0 0.0 copy-start
  15.0 0.0 copy-start.2
  15.0 0.0 copy-start.3
  15.0 20.7 %all_to_all.15 = bf16[4,1024,256]{2,1,0:T(8,128)(2,1)S(1)} all-to-all(bf16[4,1024,256]{2,1,0:T(8,128)(2,1)S(1)} %broadcast_in_dim.2), channel_id=1, replica_groups={{0,2,4,6},{8,10,12,14},{16,18,20,22},{24,26,28,30},{1,9,17,25},{3,11,19..., dimensions={0} | all-to-all | bytes 4194304 | tf_op jit(solution)/shard_map/all_to_all | solution.py:302
  35.7 0.0 copy-start.1
  35.7 0.0 collective-permute-start
  35.7 0.0 copy-done
  35.8 0.0 copy-done.2
  35.8 0.0 copy-done.3
  35.8 4.0 %forward_own.1 = (s32[256]{0:T(256)S(1)}, s32[4,256]{1,0:T(4,128)S(1)}, f32[4,256]{1,0:T(4,128)S(1)}, f32[2,128,256]{2,1,0:T(8,128)S(1)}) custom-call(s32[64]{0:T(128)S(1)} %copy-done.2, s32[16]{0:T(128)S(1)} %copy-done.3, bf16[256,256]{1,0:T(8,128)(2,1)S(1)} %copy-done, bf16[4096,256]{1,0:T(8,128)(2,1)S(1)} %bitcast.4), custom_call_target="tpu_custom_call" | custom-call | flops 2000000000 | bytes 4000000 | tf_op jit(solution)/shard_map/forward_own/pallas_call | solution.py:307
  39.8 0.1 collective-permute-done.oth_hbm
  39.9 0.0 copy-done.1
  39.9 3.5 %other_plane.1 = (bf16[256,256]{1,0:T(8,128)(2,1)}, f32[4,256]{1,0:T(4,128)S(1)}, f32[2,128,256]{2,1,0:T(8,128)S(1)}, bf16[4096,256]{1,0:T(8,128)(2,1)S(1)}) custom-call(s32[256]{0:T(256)S(1)} %get-tuple-element.14.meta, s32[4,256]{1,0:T(4,128)S(1)} %get-tuple-element.15.vec, f32[4,256]{1,0:T(4,128)S(1)} %get-tuple-element.16.stat, ...), custom_call_target="tpu_custom_call" | custom-call | flops 4000000000 | bytes 6000000 | tf_op jit(solution)/shard_map/other_plane/pallas_call | solution.py:317
  43.4 3.8 %collective-permute-start.1 = (bf16[4096,256]{1,0:T(8,128)(2,1)S(1)}, bf16[4096,256]{1,0:T(8,128)(2,1)S(1)}, u32[]{:S(2)}, u32[]{:S(2)}) collective-permute-start(bf16[4096,256]{1,0:T(8,128)(2,1)S(1)} %get-tuple-element.23), channel_id=1, source_target_pairs={{0,1},{1,0},{2,3},{3,2},{4,5},{5,4},{6,7},{7,6},{8,9},{9,8},{10,11... | collective-permute-start | bytes 6291464 | tf_op jit(solution)/shard_map/ppermute | solution.py:327
  47.2 3.6 %backward_own.1 = (bf16[256,256]{1,0:T(8,128)(2,1)}, bf16[4096,256]{1,0:T(8,128)(2,1)S(1)}) custom-call(s32[256]{0:T(256)S(1)} %get-tuple-element.14.meta, s32[4,256]{1,0:T(4,128)S(1)} %get-tuple-element.15.vec, f32[4,256]{1,0:T(4,128)S(1)} %get-tuple-element.19.lse, bf16[256,256]{1,0:T(8,128)(2,1)S(1)} %copy-done, bf16[256,256]{1,0:T(8,128)(2,1)S(1)} %copy-done.1, ...), custom_call_target="tpu_custom_call" | custom-call | flops 3000000000 | bytes 6000000 | tf_op jit(solution)/shard_map/backward_own/pallas_call | solution.py:328
  50.9 0.2 collective-permute-done.1
  51.0 0.6 add_convert_fusion
  51.6 19.0 %all_to_all.16 = bf16[4,1024,256]{2,1,0:T(8,128)(2,1)S(1)} all-to-all(bf16[4,1024,256]{2,1,0:T(8,128)(2,1)S(1)} %bitcast.6), channel_id=1, replica_groups={{0,2,4,6},{8,10,12,14},{16,18,20,22},{24,26,28,30},{1,9,17,25},{3,11,19..., dimensions={0} | all-to-all | bytes 4194304 | tf_op jit(solution)/shard_map/all_to_all | solution.py:340
  70.6 0.6 reduce_sum.24
  71.3 11.5 %all_to_all.17 = bf16[4,256,256]{2,1,0:T(8,128)(2,1)S(1)} all-to-all(bf16[4,256,256]{2,1,0:T(8,128)(2,1)S(1)} %bitcast.7), channel_id=1, replica_groups={{0,8,16,24},{2,10,18,26},{4,12,20,28},{6,14,22,30},{1,3,5,7},{9,11,13,1..., dimensions={0} | all-to-all | bytes 1048576 | tf_op jit(solution)/shard_map/all_to_all | solution.py:342
  82.7 0.1 reduce_sum.25
  82.8 0.7 fusion
Async XLA Ops:
  15.0 20.8 %copy-start = (bf16[256,256]{1,0:T(8,128)(2,1)S(1)}, bf16[256,256]{1,0:T(8,128)(2,1)}, u32[]{:S(2)}) copy-start(bf16[256,256]{1,0:T(8,128)(2,1)} %q_ref.5) | copy-start | bytes 393220
  15.0 20.8 %copy-start.2 = (s32[64]{0:T(128)S(1)}, s32[64]{0:T(128)}, u32[]{:S(2)}) copy-start(s32[64]{0:T(128)} %order.1) | copy-start | bytes 772
  15.0 20.8 %copy-start.3 = (s32[16]{0:T(128)S(1)}, s32[16]{0:T(128)}, u32[]{:S(2)}) copy-start(s32[16]{0:T(128)} %lengths.1) | copy-start | bytes 196
  35.7 4.2 %copy-start.1 = (bf16[256,256]{1,0:T(8,128)(2,1)S(1)}, bf16[256,256]{1,0:T(8,128)(2,1)}, u32[]{:S(2)}) copy-start(bf16[256,256]{1,0:T(8,128)(2,1)} %g_ref.3) | copy-start | bytes 393220
  35.7 4.2 %collective-permute-start = (bf16[4096,256]{1,0:T(8,128)(2,1)S(1)}, bf16[4096,256]{1,0:T(8,128)(2,1)S(1)}, u32[]{:S(2)}, u32[]{:S(2)}) collective-permute-start(bf16[4096,256]{1,0:T(8,128)(2,1)S(1)} %bitcast.3), channel_id=1, source_target_pairs={{0,1},{1,0},{2,3},{3,2},{4,5},{5,4},{6,7},{7,6},{8,9},{9,8},{10,11... | collective-permute-start | bytes 6291464 | tf_op jit(solution)/shard_map/ppermute | solution.py:304
  43.4 7.6 %collective-permute-start.1 = (bf16[4096,256]{1,0:T(8,128)(2,1)S(1)}, bf16[4096,256]{1,0:T(8,128)(2,1)S(1)}, u32[]{:S(2)}, u32[]{:S(2)}) collective-permute-start(bf16[4096,256]{1,0:T(8,128)(2,1)S(1)} %get-tuple-element.23), channel_id=1, source_target_pairs={{0,1},{1,0},{2,3},{3,2},{4,5},{5,4},{6,7},{7,6},{8,9},{9,8},{10,11... | collective-permute-start | bytes 6291464 | tf_op jit(solution)/shard_map/ppermute | solution.py:327

commit v4 on v3

--- a/solution.py
+++ b/solution.py
@@ -21,6 +21,7 @@
 SCALE = HD**-0.5
 SCALE2 = SCALE * 1.4426950408889634
 LANES = 2 * BLK
+LIFT = 4096.0
 
 NT = (((1,), (1,)), ((), ()))
 NN = (((1,), (0,)), ((), ()))
@@ -297,10 +298,10 @@
     scores = pltpu.VMEM((2, LIST * BLK, LANES), f32)
     sem = pltpu.SemaphoreType.DMA
     kv = jnp.concatenate([key_rows, value_rows], axis=1)
+    kv = (kv.astype(f32) * LIFT).astype(jnp.float16)
     line = lax.all_gather(kv, "ctx", axis=0, tiled=True, axis_index_groups=FIRST)
-    spread = jnp.broadcast_to(line[None], (SIDE,) + line.shape)
-    own = lax.all_to_all(spread, "ctx", 0, 0, tiled=True, axis_index_groups=SECOND)
-    own = own.reshape(plane, 2 * HD)
+    own = lax.all_gather(line, "ctx", axis=0, tiled=True, axis_index_groups=SECOND)
+    own = (own.astype(f32) * (1 / LIFT)).astype(bf16)
     oth = lax.ppermute(own, "ctx", SWAP)
     wide = shape(2, HD, LANES, dtype=f32)
     small = shape(4, LANES, dtype=f32)

time: 84.8 us -> 80.2 us (0.946)
  the two profiles are of different devices: /device:TPU:128 before, /device:TPU:160 now
where the time goes in v4:
time: 80.2 us; the launch traced here: 79.2 us
  blocking collectives  61.6 us (77%)
  Pallas kernels  9.03 us (11%)
  other arithmetic  2.81 us (4%)
  waiting for transfers between devices  2.19 us (3%)
  starting transfers between devices  1.98 us (2%)
  local copies, waits for them, and re-layouts  0.88 us (1%)
    all_to_all x1, blocking collectives, per_device(): lax.all_to_all(part, 'ctx', 0, 0, tiled=True, axis_index_groups=SECOND)  19.4 us
    all_gather x1, blocking collectives, per_device(): lax.all_gather(line, 'ctx', axis=0, tiled=True, axis_index_groups=SECOND)  16.3 us
    all_gather x1, blocking collectives, per_device(): lax.all_gather(kv, 'ctx', axis=0, tiled=True, axis_index_groups=FIRST)  13.3 us
    all_to_all x1, blocking collectives, per_device(): lax.all_to_all(part, 'ctx', 0, 0, tiled=True, axis_index_groups=FIRST)  12.6 us
    pallas_call x1, Pallas kernels, per_device(): kernel(second_pass, 'other_plane', [SMEM, VMEM, VMEM, VMEM, VMEM, VMEM, A...  3.52 us
    pallas_call x1, Pallas kernels, per_device(): kernel(first_pass, 'forward_own', [SMEM, SMEM, VMEM, ANY], (shape(META, d...  2.88 us
    pallas_call x1, Pallas kernels, per_device(): kernel(third_pass, 'backward_own', [SMEM, VMEM, VMEM, VMEM, VMEM, VMEM, A...  2.63 us
    ppermute x1, starting transfers between devices, per_device(): back = lax.ppermute(dkv_oth, 'ctx', SWAP)  1.89 us
  transfers between devices with their start and end apart: 2, of which 2 were waited for; matrix products, arithmetic and copies ran while one was open for 0% of the time, Pallas kernels for 7%

profile of v4, /device:TPU:160, one launch (start us, length us, event | category | flops | bytes accessed | tf_op | source)
XLA Modules:
  0.0 79.2 jit_solution(7289990575848347796)
XLA Ops:
  0.6 0.9 %multiply_convert_fusion.1 = f16[256,256]{1,0:T(8,128)(2,1)S(1)} fusion(bf16[256,128]{1,0:T(8,128)(2,1)} %param.8, bf16[256,128]{1,0:T(8,128)(2,1)} %param.7), kind=kLoop, calls=%fused_computation.2 | loop fusion | flops 393216 | bytes 262144 | tf_op jit(solution)/shard_map/convert_element_type | solution.py:301
  1.5 13.3 %all_gather.6 = f16[1024,256]{1,0:T(8,128)(2,1)S(1)} all-gather(f16[256,256]{1,0:T(8,128)(2,1)S(1)} %multiply_convert_fusion.1), channel_id=1, replica_groups={{0,8,16,24},{2,10,18,26},{4,12,20,28},{6,14,22,30},{1,3,5,7},{9,11,13,1..., dimensions={0}, use_global_device_ids=true | all-gather | bytes 655360 | tf_op jit(solution)/shard_map/all_gather | solution.py:302
  14.8 16.3 %all-gather.1 = f16[4096,256]{1,0:T(8,128)(2,1)S(1)} all-gather(f16[1024,256]{1,0:T(8,128)(2,1)S(1)} %all_gather.6), channel_id=1, replica_groups={{0,2,4,6},{8,10,12,14},{16,18,20,22},{24,26,28,30},{1,9,17,25},{3,11,19..., dimensions={0}, use_global_device_ids=true | all-gather | bytes 2621440 | tf_op jit(solution)/shard_map/all_gather | solution.py:303
  31.1 0.0 copy-start
  31.1 0.0 copy-start.2
  31.1 0.0 copy-start.3
  31.1 0.6 multiply_convert_fusion.own_hbm
  31.7 0.0 copy-start.1
  31.7 0.1 collective-permute-start
  31.8 0.2 copy-done
  32.0 0.0 copy-done.2
  32.0 0.0 copy-done.3
  32.0 2.9 %forward_own.1 = (s32[256]{0:T(256)S(1)}, s32[4,256]{1,0:T(4,128)S(1)}, f32[4,256]{1,0:T(4,128)S(1)}, f32[2,128,256]{2,1,0:T(8,128)S(1)}) custom-call(s32[64]{0:T(128)S(1)} %copy-done.2, s32[16]{0:T(128)S(1)} %copy-done.3, bf16[256,256]{1,0:T(8,128)(2,1)S(1)} %copy-done, bf16[4096,256]{1,0:T(8,128)(2,1)S(1)} %multiply_convert_fusion.own_hbm), custom_call_target="tpu_custom_call" | custom-call | flops 2000000000 | bytes 4000000 | tf_op jit(solution)/shard_map/forward_own/pallas_call | solution.py:308
  34.9 1.0 %collective-permute-done.oth_hbm = bf16[4096,256]{1,0:T(8,128)(2,1)S(1)} collective-permute-done((bf16[4096,256]{1,0:T(8,128)(2,1)S(1)}, bf16[4096,256]{1,0:T(8,128)(2,1)S(1)}, u32[]{:S(2)}, u32[]{:S(2)}) %collective-permute-start) | collective-permute-done | bytes 2097184 | tf_op jit(solution)/shard_map/ppermute | solution.py:305
  36.0 0.0 copy-done.1
  36.0 3.5 %other_plane.1 = (bf16[256,256]{1,0:T(8,128)(2,1)}, f32[4,256]{1,0:T(4,128)S(1)}, f32[2,128,256]{2,1,0:T(8,128)S(1)}, bf16[4096,256]{1,0:T(8,128)(2,1)S(1)}) custom-call(s32[256]{0:T(256)S(1)} %get-tuple-element.14.meta, s32[4,256]{1,0:T(4,128)S(1)} %get-tuple-element.15.vec, f32[4,256]{1,0:T(4,128)S(1)} %get-tuple-element.16.stat, ...), custom_call_target="tpu_custom_call" | custom-call | flops 4000000000 | bytes 6000000 | tf_op jit(solution)/shard_map/other_plane/pallas_call | solution.py:318
  39.5 1.9 %collective-permute-start.1 = (bf16[4096,256]{1,0:T(8,128)(2,1)S(1)}, bf16[4096,256]{1,0:T(8,128)(2,1)S(1)}, u32[]{:S(2)}, u32[]{:S(2)}) collective-permute-start(bf16[4096,256]{1,0:T(8,128)(2,1)S(1)} %get-tuple-element.23), channel_id=1, source_target_pairs={{0,1},{1,0},{2,3},{3,2},{4,5},{5,4},{6,7},{7,6},{8,9},{9,8},{10,11... | collective-permute-start | bytes 6291464 | tf_op jit(solution)/shard_map/ppermute | solution.py:328
  41.4 2.6 %backward_own.1 = (bf16[256,256]{1,0:T(8,128)(2,1)}, bf16[4096,256]{1,0:T(8,128)(2,1)S(1)}) custom-call(s32[256]{0:T(256)S(1)} %get-tuple-element.14.meta, s32[4,256]{1,0:T(4,128)S(1)} %get-tuple-element.15.vec, f32[4,256]{1,0:T(4,128)S(1)} %get-tuple-element.19.lse, bf16[256,256]{1,0:T(8,128)(2,1)S(1)} %copy-done, bf16[256,256]{1,0:T(8,128)(2,1)S(1)} %copy-done.1, ...), custom_call_target="tpu_custom_call" | custom-call | flops 3000000000 | bytes 6000000 | tf_op jit(solution)/shard_map/backward_own/pallas_call | solution.py:329
  44.0 1.1 %collective-permute-done.1 = bf16[4096,256]{1,0:T(8,128)(2,1)S(1)} collective-permute-done((bf16[4096,256]{1,0:T(8,128)(2,1)S(1)}, bf16[4096,256]{1,0:T(8,128)(2,1)S(1)}, u32[]{:S(2)}, u32[]{:S(2)}) %collective-permute-start.1) | collective-permute-done | bytes 2097184 | tf_op jit(solution)/shard_map/ppermute | solution.py:328
  45.2 0.6 add_convert_fusion
  45.8 19.4 %all_to_all.10 = bf16[4,1024,256]{2,1,0:T(8,128)(2,1)S(1)} all-to-all(bf16[4,1024,256]{2,1,0:T(8,128)(2,1)S(1)} %bitcast.2), channel_id=1, replica_groups={{0,2,4,6},{8,10,12,14},{16,18,20,22},{24,26,28,30},{1,9,17,25},{3,11,19..., dimensions={0} | all-to-all | bytes 4194304 | tf_op jit(solution)/shard_map/all_to_all | solution.py:341
  65.2 0.6 reduce_sum.24
  65.8 12.6 %all_to_all.11 = bf16[4,256,256]{2,1,0:T(8,128)(2,1)S(1)} all-to-all(bf16[4,256,256]{2,1,0:T(8,128)(2,1)S(1)} %bitcast.3), channel_id=1, replica_groups={{0,8,16,24},{2,10,18,26},{4,12,20,28},{6,14,22,30},{1,3,5,7},{9,11,13,1..., dimensions={0} | all-to-all | bytes 1048576 | tf_op jit(solution)/shard_map/all_to_all | solution.py:343
  78.4 0.1 reduce_sum.25
  78.5 0.7 fusion
Async XLA Ops:
  31.1 0.9 %copy-start = (bf16[256,256]{1,0:T(8,128)(2,1)S(1)}, bf16[256,256]{1,0:T(8,128)(2,1)}, u32[]{:S(2)}) copy-start(bf16[256,256]{1,0:T(8,128)(2,1)} %q_ref.5) | copy-start | bytes 393220
  31.1 0.9 %copy-start.2 = (s32[64]{0:T(128)S(1)}, s32[64]{0:T(128)}, u32[]{:S(2)}) copy-start(s32[64]{0:T(128)} %order.1) | copy-start | bytes 772
  31.1 0.9 %copy-start.3 = (s32[16]{0:T(128)S(1)}, s32[16]{0:T(128)}, u32[]{:S(2)}) copy-start(s32[16]{0:T(128)} %lengths.1) | copy-start | bytes 196
  31.7 4.3 %copy-start.1 = (bf16[256,256]{1,0:T(8,128)(2,1)S(1)}, bf16[256,256]{1,0:T(8,128)(2,1)}, u32[]{:S(2)}) copy-start(bf16[256,256]{1,0:T(8,128)(2,1)} %g_ref.3) | copy-start | bytes 393220
  31.7 4.2 %collective-permute-start = (bf16[4096,256]{1,0:T(8,128)(2,1)S(1)}, bf16[4096,256]{1,0:T(8,128)(2,1)S(1)}, u32[]{:S(2)}, u32[]{:S(2)}) collective-permute-start(bf16[4096,256]{1,0:T(8,128)(2,1)S(1)} %multiply_convert_fusion.own_hbm), channel_id=1, source_target_pairs={{0,1},{1,0},{2,3},{3,2},{4,5},{5,4},{6,7},{7,6},{8,9},{9,8},{10,11... | collective-permute-start | bytes 6291464 | tf_op jit(solution)/shard_map/ppermute | solution.py:305
  39.5 5.7 %collective-permute-start.1 = (bf16[4096,256]{1,0:T(8,128)(2,1)S(1)}, bf16[4096,256]{1,0:T(8,128)(2,1)S(1)}, u32[]{:S(2)}, u32[]{:S(2)}) collective-permute-start(bf16[4096,256]{1,0:T(8,128)(2,1)S(1)} %get-tuple-element.23), channel_id=1, source_target_pairs={{0,1},{1,0},{2,3},{3,2},{4,5},{5,4},{6,7},{7,6},{8,9},{9,8},{10,11... | collective-permute-start | bytes 6291464 | tf_op jit(solution)/shard_map/ppermute | solution.py:328

commit v5 on v4

v5 whole, which is shorter than its diff:
```python
import jax
import jax.numpy as jnp
from jax import lax
from jax.experimental import pallas as pl
from jax.experimental.pallas import tpu as pltpu
from jax.sharding import PartitionSpec as P

BLK = 128
HD = 128
NBLK = 64
NDOC = 16
SIDE = 4
HALF = NBLK // 2
CHUNK = 4
REACH = 17
LIST = 48
ROWS_AT = 2 * LIST
COUNT_AT = 4 * LIST
META = 256
NEG = -1e30
SCALE = HD**-0.5
SCALE2 = SCALE * 1.4426950408889634
LANES = 2 * BLK
LIFT = 4096.0

NT = (((1,), (1,)), ((), ()))
NN = (((1,), (0,)), ((), ()))
TN = (((0,), (0,)), ((), ()))
KEYS, VALS = slice(0, HD), slice(HD, 2 * HD)


def device_of(y, x, core):
    return (y % SIDE) * 2 * SIDE + (x % SIDE) * 2 + core


def along(axis_of_core):
    groups = []
    for core in range(2):
        for fixed in range(SIDE):
            if axis_of_core[core] == "y":
                groups.append([device_of(i, fixed, core) for i in range(SIDE)])
            else:
                groups.append([device_of(fixed, i, core) for i in range(SIDE)])
    return groups


FIRST = along("yx")
SECOND = along("xy")
SWAP = [(i, i ^ 1) for i in range(2 * SIDE * SIDE)]


def mm(a, b, dims):
    return lax.dot_general(a, b, dims, preferred_element_type=jnp.float32)


def stacked(ref, i):
    rows = pl.ds(i * BLK, BLK)
    return jnp.concatenate([ref[rows, :HD], ref[rows, HD:]], axis=0)


def unstack(ref, i, value):
    rows = pl.ds(i * BLK, BLK)
    ref[rows, :HD] = value[:BLK]
    ref[rows, HD:] = value[BLK:]


def load(kv, meta, plane, ch, cols):
    return jnp.concatenate([kv[pl.ds(row_of(meta, plane, ch, j), BLK), cols] for j in range(CHUNK)], axis=0)


def row_of(meta, plane, ch, j):
    return pl.multiple_of(meta[ROWS_AT + plane * LIST + ch * CHUNK + j] * BLK, BLK)


def scores_of(keys, q, meta, vec, plane, ch, i):
    s = mm(keys, q, NT)
    sub = lax.broadcasted_iota(jnp.int32, (BLK, LANES), 0)
    qstart, qpos = vec[pl.ds(2 * i, 1), :], vec[pl.ds(2 * i + 1, 1), :]
    parts = []
    for j in range(CHUNK):
        first = meta[plane * LIST + ch * CHUNK + j] * BLK
        ok = (sub >= qstart - first) & (sub <= qpos - first)
        parts.append(jnp.where(ok, s[j * BLK : (j + 1) * BLK], NEG))
    return jnp.concatenate(parts, axis=0)


def each_chunk(meta, plane, body):
    split, total = meta[COUNT_AT + 2 * plane], meta[COUNT_AT + 2 * plane + 1]

    def pair(t, _):
        for ch in (2 * t, 2 * t + 1):
            body(ch, jnp.where(ch >= split, 1, 0))
        return 0

    lax.fori_loop(0, total >> 1, pair, 0)

    @pl.when((total & 1) == 1)
    def _():
        body(total - 1, jnp.where(total > split, 1, 0))


def chunk_at(ch):
    return pl.ds(pl.multiple_of(ch * CHUNK * BLK, CHUNK * BLK), CHUNK * BLK)


def forward(meta, vec, plane, kv, q_st, top, total, out, s_ref, p_ref, old_top=None):
    def scores(ch, i):
        s = scores_of(load(kv, meta, plane, ch, KEYS), q_st[i], meta, vec, plane, ch, i)
        s_ref[chunk_at(ch), :] = s
        row = pl.ds(i, 1)
        top[row, :] = jnp.maximum(top[row, :], jnp.max(s, axis=0, keepdims=True))

    each_chunk(meta, plane, scores)
    if old_top is not None:
        for i in range(2):
            row = slice(i, i + 1)
            shrink = jnp.exp2((old_top[i] - top[row, :]) * SCALE2)
            total[row, :] = total[row, :] * shrink
            out[i] = out[i] * shrink

    def outputs(ch, i):
        row = pl.ds(i, 1)
        p = jnp.exp2((s_ref[chunk_at(ch), :] - top[row, :]) * SCALE2)
        total[row, :] = total[row, :] + jnp.sum(p, axis=0, keepdims=True)
        p = p.astype(jnp.bfloat16)
        if p_ref is not None:
            p_ref[chunk_at(ch), :] = p
        out[i] = out[i] + mm(load(kv, meta, plane, ch, VALS), p, TN)

    each_chunk(meta, plane, outputs)


def first_pass(order, lengths, q_ref, own_hbm, meta, vec, stat, part, kv, q_st, s_ref, top, total, table, sem):
    copy = fetch_all(own_hbm, kv, sem)
    me = lax.axis_index("ctx")
    core = me & 1
    for s in range(NBLK):
        dev = s // 2
        y, x, c = dev // (2 * SIDE), (dev // 2) % SIDE, dev % 2
        slot = (y * SIDE + x if c else x * SIDE + y) * 2 + s % 2
        table[order[s]] = slot + (HALF * (1 - core) if c else HALF * core)
    lane = lax.broadcasted_iota(jnp.int32, (1, LANES), 1) & (BLK - 1)
    mine, others = jnp.int32(0), jnp.int32(LIST)
    for i in range(2):
        blk = order[2 * me + i]
        qpos = blk * BLK + lane
        end, low = jnp.int32(0), jnp.int32(0)
        qstart = jnp.zeros((1, LANES), jnp.int32)
        for d in range(NDOC):
            end = end + lengths[d]
            qstart = jnp.where(qpos >= end, end, qstart)
            low = jnp.where(blk * BLK >= end, end, low)
        vec[2 * i : 2 * i + 1, :] = qstart
        vec[2 * i + 1 : 2 * i + 2, :] = qpos
        low = low >> 7
        for j in range(REACH):
            p = blk - j
            slot = table[jnp.maximum(p, 0)]
            away = slot >= HALF
            at = jnp.where(away, others, mine)
            meta[at] = p
            meta[ROWS_AT + at] = slot & (HALF - 1)
            step = jnp.where(p >= low, 1, 0)
            others = others + jnp.where(away, step, 0)
            mine = mine + jnp.where(away, 0, step)
        for j in range(CHUNK - 1):
            for at in (mine, others):
                meta[at + j] = -1024
                meta[ROWS_AT + at + j] = 0
        mine = (mine + CHUNK - 1) // CHUNK * CHUNK
        others = (others + CHUNK - 1) // CHUNK * CHUNK
        meta[COUNT_AT + i] = mine // CHUNK
        meta[COUNT_AT + 2 + i] = (others - LIST) // CHUNK
        q_st[i] = stacked(q_ref, i)
    top[...] = jnp.full_like(top, NEG)
    total[...] = jnp.zeros_like(total)
    part[...] = jnp.zeros_like(part)
    copy.wait()
    forward(meta, vec, 0, kv, q_st, top, total, part, s_ref, None)
    stat[pl.ds(0, 2), :] = top[...]
    stat[pl.ds(2, 2), :] = total[...]


def fetch_all(hbm, kv, sem):
    copy = pltpu.make_async_copy(hbm, kv, sem)
    copy.start()
    return copy


def put(ref, meta, plane, ch, dk, dv):
    for j in range(CHUNK):
        to = pl.ds(row_of(meta, plane, ch, j), BLK)
        rows = slice(j * BLK, (j + 1) * BLK)
        ref[to, KEYS] = (ref[to, KEYS].astype(jnp.float32) + dk[rows]).astype(jnp.bfloat16)
        ref[to, VALS] = (ref[to, VALS].astype(jnp.float32) + dv[rows]).astype(jnp.bfloat16)


def second_pass(
    meta, vec, stat, q_ref, g_ref, part, oth_hbm, o_ref, lse, dq_ref, dkv,
    kv, q_st, g_st, over, s_ref, p_ref, top, total, out, scaled, sem
):
    copy = fetch_all(oth_hbm, kv, sem)
    dkv[...] = jnp.zeros_like(dkv)
    dq_ref[...] = jnp.zeros_like(dq_ref)
    for i in range(2):
        q_st[i], g_st[i] = stacked(q_ref, i), stacked(g_ref, i)
    top[...] = stat[pl.ds(0, 2), :]
    total[...] = stat[pl.ds(2, 2), :]
    out[...] = part[...]
    copy.wait()
    forward(meta, vec, 1, kv, q_st, top, total, out, s_ref, p_ref, [stat[i : i + 1, :] for i in range(2)])
    for i in range(2):
        row = slice(i, i + 1)
        inv = 1.0 / total[row, :]
        att = (out[i] * inv).T.astype(jnp.bfloat16)
        unstack(o_ref, i, att)
        wide = g_st[i].astype(jnp.float32)
        lse[i : i + 1, :] = top[row, :] * SCALE2 + jnp.log2(total[row, :])
        lse[2 + i : 3 + i, :] = jnp.sum((wide * att.astype(jnp.float32)).T, axis=0, keepdims=True)
        scaled[row, :] = inv * SCALE
        over[i] = (wide * jnp.broadcast_to(inv, (HD, LANES)).T).astype(jnp.bfloat16)

    def grads(ch, i):
        p = p_ref[chunk_at(ch), :]
        dp = mm(load(kv, meta, 1, ch, VALS), g_st[i], NT)
        ds = ((p.astype(jnp.float32) * scaled[pl.ds(i, 1), :]) * (dp - lse[pl.ds(2 + i, 1), :])).astype(jnp.bfloat16)
        put(dkv, meta, 1, ch, mm(ds, q_st[i], NN), mm(p, over[i], NN))
        dq_ref[i] = dq_ref[i] + mm(load(kv, meta, 1, ch, KEYS), ds, TN)

    each_chunk(meta, 1, grads)


def third_pass(meta, vec, lse, q_ref, g_ref, dq_in, own_hbm, dq_ref, dkv, kv, q_st, g_st, dq, sem):
    copy = fetch_all(own_hbm, kv, sem)
    dkv[...] = jnp.zeros_like(dkv)
    dq[...] = dq_in[...]
    for i in range(2):
        q_st[i], g_st[i] = stacked(q_ref, i), stacked(g_ref, i)
    copy.wait()

    def grads(ch, i):
        keys = load(kv, meta, 0, ch, KEYS)
        s = scores_of(keys, q_st[i], meta, vec, 0, ch, i)
        p = jnp.exp2(s * SCALE2 - lse[pl.ds(i, 1), :])
        dp = mm(load(kv, meta, 0, ch, VALS), g_st[i], NT)
        ds = ((p * SCALE) * (dp - lse[pl.ds(2 + i, 1), :])).astype(jnp.bfloat16)
        put(dkv, meta, 0, ch, mm(ds, q_st[i], NN), mm(p.astype(jnp.bfloat16), g_st[i], NN))
        dq[i] = dq[i] + mm(keys, ds, TN)

    each_chunk(meta, 0, grads)
    for i in range(2):
        unstack(dq_ref, i, dq[i].T.astype(jnp.bfloat16))


SMEM = pl.BlockSpec(memory_space=pltpu.SMEM)
VMEM = pl.BlockSpec(memory_space=pltpu.VMEM)
ANY = pl.BlockSpec(memory_space=pl.ANY)


def shape(*dims, dtype=jnp.bfloat16):
    return jax.ShapeDtypeStruct(dims, dtype)


def kernel(body, name, ins, outs, out_specs, scratch, flops, size):
    return pl.pallas_call(
        body,
        out_shape=outs,
        in_specs=ins,
        out_specs=out_specs,
        scratch_shapes=scratch,
        compiler_params=pltpu.CompilerParams(vmem_limit_bytes=48 * 1024 * 1024),
        cost_estimate=pl.CostEstimate(flops=flops, bytes_accessed=size, transcendentals=0),
        name=name,
    )


def per_device(queries, key_rows, value_rows, grad_output, doc_lengths, block_order):
    tokens = queries.shape[0]
    f32, i32, bf16 = jnp.float32, jnp.int32, jnp.bfloat16
    plane = HALF * BLK
    padded = pltpu.VMEM((plane, 2 * HD), bf16)
    scores = pltpu.VMEM((LIST * BLK, LANES), f32)
    weights = pltpu.VMEM((LIST * BLK, LANES), bf16)
    rows = pltpu.VMEM((2, LANES, HD), bf16)
    pair = pltpu.VMEM((2, LANES), f32)
    sums = pltpu.VMEM((2, HD, LANES), f32)
    sem = pltpu.SemaphoreType.DMA
    kv = jnp.concatenate([key_rows, value_rows], axis=1)
    kv = (kv.astype(f32) * LIFT).astype(jnp.float16)
    line = lax.all_gather(kv, "ctx", axis=0, tiled=True, axis_index_groups=FIRST)
    own = lax.all_gather(line, "ctx", axis=0, tiled=True, axis_index_groups=SECOND)
    own = (own.astype(f32) * (1 / LIFT)).astype(bf16)
    oth = lax.ppermute(own, "ctx", SWAP)
    wide = shape(2, HD, LANES, dtype=f32)
    small = shape(4, LANES, dtype=f32)
    meta, vec, stat, part = kernel(
        first_pass,
        "forward_own",
        [SMEM, SMEM, VMEM, ANY],
        (shape(META, dtype=i32), shape(4, LANES, dtype=i32), small, wide),
        (SMEM, VMEM, VMEM, VMEM),
        [padded, rows, scores, pair, pair, pltpu.SMEM((NBLK,), i32), sem],
        2 * 10**9,
        4 * 10**6,
    )(block_order, doc_lengths, queries, own)
    attention, lse, dq, dkv_oth = kernel(
        second_pass,
        "other_plane",
        [SMEM, VMEM, VMEM, VMEM, VMEM, VMEM, ANY],
        (shape(tokens, 2 * HD), small, wide, shape(plane, 2 * HD)),
        (VMEM,) * 4,
        [padded, rows, rows, rows, scores, weights, pair, pair, sums, pair, sem],
        4 * 10**9,
        6 * 10**6,
    )(meta, vec, stat, queries, grad_output, part, oth)
    back = lax.ppermute(dkv_oth, "ctx", SWAP)
    grad_queries, dkv_own = kernel(
        third_pass,
        "backward_own",
        [SMEM, VMEM, VMEM, VMEM, VMEM, VMEM, ANY],
        (shape(tokens, 2 * HD), shape(plane, 2 * HD)),
        (VMEM,) * 2,
        [padded, rows, rows, sums, sem],
        3 * 10**9,
        6 * 10**6,
    )(meta, vec, lse, queries, grad_output, dq, own)
    part = (dkv_own.astype(f32) + back.astype(f32)).astype(bf16)
    part = part.reshape(SIDE, SIDE * tokens, 2 * HD)
    part = lax.all_to_all(part, "ctx", 0, 0, tiled=True, axis_index_groups=SECOND)
    part = jnp.sum(part.astype(f32), axis=0).astype(bf16).reshape(SIDE, tokens, 2 * HD)
    part = lax.all_to_all(part, "ctx", 0, 0, tiled=True, axis_index_groups=FIRST)
    part = jnp.sum(part.astype(f32), axis=0).astype(bf16)
    return attention, grad_queries, part[:, :HD], part[:, HD:]


def solution(mesh):
    rows = P(("dp", "ctx"), None)
    return jax.shard_map(
        per_device,
        mesh=mesh,
        in_specs=(rows, rows, rows, rows, P("dp"), P("dp")),
        out_specs=(rows, rows, rows, rows),
        check_vma=False,
    )
```

time: 80.2 us -> 79.2 us (0.988)
  waiting for transfers between devices: 2.19 us -> 0.81 us
    ppermute x1, waiting for transfers between devices: 1.15 us -> 0.21 us  [per_device(): back = lax.ppermute(dkv_oth, 'ctx', SWAP)]
    pallas_call x1, Pallas kernels: 2.63 us -> 3.57 us  [per_device(): kernel(third_pass, 'backward_own', [SMEM, VMEM, VMEM, VMEM, VMEM, VMEM, A...]
  transfers between devices with their start and end apart: 2 -> 2, of which waited for: 2 -> 2; matrix products, arithmetic and copies ran while one was open for 0% -> 0% of each run, Pallas kernels for 7% -> 9%
where the time goes in v5:
time: 79.2 us; the launch traced here: 77.8 us
  blocking collectives  60.9 us (77%)
  Pallas kernels  9.79 us (12%)
  other arithmetic  2.81 us (4%)
  starting transfers between devices  1.96 us (2%)
  local copies, waits for them, and re-layouts  0.88 us (1%)
  waiting for transfers between devices  0.81 us (1%)
    all_to_all x1, blocking collectives, per_device(): lax.all_to_all(part, 'ctx', 0, 0, tiled=True, axis_index_groups=SECOND)  19 us
    all_gather x1, blocking collectives, per_device(): lax.all_gather(line, 'ctx', axis=0, tiled=True, axis_index_groups=SECOND)  16.3 us
    all_gather x1, blocking collectives, per_device(): lax.all_gather(kv, 'ctx', axis=0, tiled=True, axis_index_groups=FIRST)  13.3 us
    all_to_all x1, blocking collectives, per_device(): lax.all_to_all(part, 'ctx', 0, 0, tiled=True, axis_index_groups=FIRST)  12.3 us
    pallas_call x1, Pallas kernels, per_device(): kernel(third_pass, 'backward_own', [SMEM, VMEM, VMEM, VMEM, VMEM, VMEM, A...  3.57 us
    pallas_call x1, Pallas kernels, per_device(): kernel(first_pass, 'forward_own', [SMEM, SMEM, VMEM, ANY], (shape(META, d...  3.32 us
    pallas_call x1, Pallas kernels, per_device(): kernel(second_pass, 'other_plane', [SMEM, VMEM, VMEM, VMEM, VMEM, VMEM, A...  2.9 us
    ppermute x1, starting transfers between devices, per_device(): back = lax.ppermute(dkv_oth, 'ctx', SWAP)  1.87 us
  transfers between devices with their start and end apart: 2, of which 2 were waited for; matrix products, arithmetic and copies ran while one was open for 0% of the time, Pallas kernels for 9%

profile of v5, /device:TPU:160, one launch (start us, length us, event | category | flops | bytes accessed | tf_op | source)
XLA Modules:
  0.0 77.8 jit_solution(11087300517844014137)
XLA Ops:
  0.6 0.9 %multiply_convert_fusion.1 = f16[256,256]{1,0:T(8,128)(2,1)S(1)} fusion(bf16[256,128]{1,0:T(8,128)(2,1)} %param.8, bf16[256,128]{1,0:T(8,128)(2,1)} %param.7), kind=kLoop, calls=%fused_computation.2 | loop fusion | flops 393216 | bytes 262144 | tf_op jit(solution)/shard_map/convert_element_type | solution.py:289
  1.5 13.3 %all_gather.6 = f16[1024,256]{1,0:T(8,128)(2,1)S(1)} all-gather(f16[256,256]{1,0:T(8,128)(2,1)S(1)} %multiply_convert_fusion.1), channel_id=1, replica_groups={{0,8,16,24},{2,10,18,26},{4,12,20,28},{6,14,22,30},{1,3,5,7},{9,11,13,1..., dimensions={0}, use_global_device_ids=true | all-gather | bytes 655360 | tf_op jit(solution)/shard_map/all_gather | solution.py:290
  14.8 16.3 %all-gather.1 = f16[4096,256]{1,0:T(8,128)(2,1)S(1)} all-gather(f16[1024,256]{1,0:T(8,128)(2,1)S(1)} %all_gather.6), channel_id=1, replica_groups={{0,2,4,6},{8,10,12,14},{16,18,20,22},{24,26,28,30},{1,9,17,25},{3,11,19..., dimensions={0}, use_global_device_ids=true | all-gather | bytes 2621440 | tf_op jit(solution)/shard_map/all_gather | solution.py:291
  31.1 0.0 copy-start
  31.1 0.0 copy-start.2
  31.1 0.0 copy-start.3
  31.1 0.6 multiply_convert_fusion.own_hbm
  31.7 0.0 copy-start.1
  31.7 0.1 collective-permute-start
  31.8 0.2 copy-done
  32.0 0.0 copy-done.2
  32.0 0.0 copy-done.3
  32.0 3.3 %forward_own.1 = (s32[256]{0:T(256)S(1)}, s32[4,256]{1,0:T(4,128)S(1)}, f32[4,256]{1,0:T(4,128)S(1)}, f32[2,128,256]{2,1,0:T(8,128)S(1)}) custom-call(s32[64]{0:T(128)S(1)} %copy-done.2, s32[16]{0:T(128)S(1)} %copy-done.3, bf16[256,256]{1,0:T(8,128)(2,1)S(1)} %copy-done, bf16[4096,256]{1,0:T(8,128)(2,1)S(1)} %multiply_convert_fusion.own_hbm), custom_call_target="tpu_custom_call" | custom-call | flops 2000000000 | bytes 4000000 | tf_op jit(solution)/shard_map/forward_own/pallas_call | solution.py:296
  35.4 0.6 collective-permute-done.oth_hbm
  36.0 0.0 copy-done.1
  36.0 2.9 %other_plane.1 = (bf16[256,256]{1,0:T(8,128)(2,1)}, f32[4,256]{1,0:T(4,128)S(1)}, f32[2,128,256]{2,1,0:T(8,128)S(1)}, bf16[4096,256]{1,0:T(8,128)(2,1)S(1)}) custom-call(s32[256]{0:T(256)S(1)} %get-tuple-element.14.meta, s32[4,256]{1,0:T(4,128)S(1)} %get-tuple-element.15.vec, f32[4,256]{1,0:T(4,128)S(1)} %get-tuple-element.16.stat, ...), custom_call_target="tpu_custom_call" | custom-call | flops 4000000000 | bytes 6000000 | tf_op jit(solution)/shard_map/other_plane/pallas_call | solution.py:306
  38.9 1.9 %collective-permute-start.1 = (bf16[4096,256]{1,0:T(8,128)(2,1)S(1)}, bf16[4096,256]{1,0:T(8,128)(2,1)S(1)}, u32[]{:S(2)}, u32[]{:S(2)}) collective-permute-start(bf16[4096,256]{1,0:T(8,128)(2,1)S(1)} %get-tuple-element.23), channel_id=1, source_target_pairs={{0,1},{1,0},{2,3},{3,2},{4,5},{5,4},{6,7},{7,6},{8,9},{9,8},{10,11... | collective-permute-start | bytes 6291464 | tf_op jit(solution)/shard_map/ppermute | solution.py:316
  40.8 3.6 %backward_own.1 = (bf16[256,256]{1,0:T(8,128)(2,1)}, bf16[4096,256]{1,0:T(8,128)(2,1)S(1)}) custom-call(s32[256]{0:T(256)S(1)} %get-tuple-element.14.meta, s32[4,256]{1,0:T(4,128)S(1)} %get-tuple-element.15.vec, f32[4,256]{1,0:T(4,128)S(1)} %get-tuple-element.19.lse, bf16[256,256]{1,0:T(8,128)(2,1)S(1)} %copy-done, bf16[256,256]{1,0:T(8,128)(2,1)S(1)} %copy-done.1, ...), custom_call_target="tpu_custom_call" | custom-call | flops 3000000000 | bytes 6000000 | tf_op jit(solution)/shard_map/backward_own/pallas_call | solution.py:317
  44.3 0.2 collective-permute-done.1
  44.5 0.6 add_convert_fusion
  45.1 19.0 %all_to_all.10 = bf16[4,1024,256]{2,1,0:T(8,128)(2,1)S(1)} all-to-all(bf16[4,1024,256]{2,1,0:T(8,128)(2,1)S(1)} %bitcast.2), channel_id=1, replica_groups={{0,2,4,6},{8,10,12,14},{16,18,20,22},{24,26,28,30},{1,9,17,25},{3,11,19..., dimensions={0} | all-to-all | bytes 4194304 | tf_op jit(solution)/shard_map/all_to_all | solution.py:329
  64.2 0.6 reduce_sum.24
  64.8 12.3 %all_to_all.11 = bf16[4,256,256]{2,1,0:T(8,128)(2,1)S(1)} all-to-all(bf16[4,256,256]{2,1,0:T(8,128)(2,1)S(1)} %bitcast.3), channel_id=1, replica_groups={{0,8,16,24},{2,10,18,26},{4,12,20,28},{6,14,22,30},{1,3,5,7},{9,11,13,1..., dimensions={0} | all-to-all | bytes 1048576 | tf_op jit(solution)/shard_map/all_to_all | solution.py:331
  77.1 0.1 reduce_sum.25
  77.2 0.7 fusion
Async XLA Ops:
  31.1 0.9 %copy-start = (bf16[256,256]{1,0:T(8,128)(2,1)S(1)}, bf16[256,256]{1,0:T(8,128)(2,1)}, u32[]{:S(2)}) copy-start(bf16[256,256]{1,0:T(8,128)(2,1)} %q_ref.5) | copy-start | bytes 393220
  31.1 0.9 %copy-start.2 = (s32[64]{0:T(128)S(1)}, s32[64]{0:T(128)}, u32[]{:S(2)}) copy-start(s32[64]{0:T(128)} %order.1) | copy-start | bytes 772
  31.1 0.9 %copy-start.3 = (s32[16]{0:T(128)S(1)}, s32[16]{0:T(128)}, u32[]{:S(2)}) copy-start(s32[16]{0:T(128)} %lengths.1) | copy-start | bytes 196
  31.7 4.3 %copy-start.1 = (bf16[256,256]{1,0:T(8,128)(2,1)S(1)}, bf16[256,256]{1,0:T(8,128)(2,1)}, u32[]{:S(2)}) copy-start(bf16[256,256]{1,0:T(8,128)(2,1)} %g_ref.3) | copy-start | bytes 393220
  31.7 4.2 %collective-permute-start = (bf16[4096,256]{1,0:T(8,128)(2,1)S(1)}, bf16[4096,256]{1,0:T(8,128)(2,1)S(1)}, u32[]{:S(2)}, u32[]{:S(2)}) collective-permute-start(bf16[4096,256]{1,0:T(8,128)(2,1)S(1)} %multiply_convert_fusion.own_hbm), channel_id=1, source_target_pairs={{0,1},{1,0},{2,3},{3,2},{4,5},{5,4},{6,7},{7,6},{8,9},{9,8},{10,11... | collective-permute-start | bytes 6291464 | tf_op jit(solution)/shard_map/ppermute | solution.py:293
  38.9 5.7 %collective-permute-start.1 = (bf16[4096,256]{1,0:T(8,128)(2,1)S(1)}, bf16[4096,256]{1,0:T(8,128)(2,1)S(1)}, u32[]{:S(2)}, u32[]{:S(2)}) collective-permute-start(bf16[4096,256]{1,0:T(8,128)(2,1)S(1)} %get-tuple-element.23), channel_id=1, source_target_pairs={{0,1},{1,0},{2,3},{3,2},{4,5},{5,4},{6,7},{7,6},{8,9},{9,8},{10,11... | collective-permute-start | bytes 6291464 | tf_op jit(solution)/shard_map/ppermute | solution.py:316

commit v6 on v5

--- a/solution.py
+++ b/solution.py
@@ -130,8 +130,7 @@
     each_chunk(meta, plane, outputs)
 
 
-def first_pass(order, lengths, q_ref, own_hbm, meta, vec, stat, part, kv, q_st, s_ref, top, total, table, sem):
-    copy = fetch_all(own_hbm, kv, sem)
+def first_pass(order, lengths, q_ref, kv, meta, vec, stat, part, q_st, s_ref, top, total, table):
     me = lax.axis_index("ctx")
     core = me & 1
     for s in range(NBLK):
@@ -175,16 +174,9 @@
     top[...] = jnp.full_like(top, NEG)
     total[...] = jnp.zeros_like(total)
     part[...] = jnp.zeros_like(part)
-    copy.wait()
     forward(meta, vec, 0, kv, q_st, top, total, part, s_ref, None)
     stat[pl.ds(0, 2), :] = top[...]
     stat[pl.ds(2, 2), :] = total[...]
-
-
-def fetch_all(hbm, kv, sem):
-    copy = pltpu.make_async_copy(hbm, kv, sem)
-    copy.start()
-    return copy
 
 
 def put(ref, meta, plane, ch, dk, dv):
@@ -196,10 +188,9 @@
 
 
 def second_pass(
-    meta, vec, stat, q_ref, g_ref, part, oth_hbm, o_ref, lse, dq_ref, dkv,
-    kv, q_st, g_st, over, s_ref, p_ref, top, total, out, scaled, sem
+    meta, vec, stat, q_ref, g_ref, part, kv, o_ref, lse, dq_ref, dkv,
+    q_st, g_st, over, s_ref, p_ref, top, total, out, scaled
 ):
-    copy = fetch_all(oth_hbm, kv, sem)
     dkv[...] = jnp.zeros_like(dkv)
     dq_ref[...] = jnp.zeros_like(dq_ref)
     for i in range(2):
@@ -207,7 +198,6 @@
     top[...] = stat[pl.ds(0, 2), :]
     total[...] = stat[pl.ds(2, 2), :]
     out[...] = part[...]
-    copy.wait()
     forward(meta, vec, 1, kv, q_st, top, total, out, s_ref, p_ref, [stat[i : i + 1, :] for i in range(2)])
     for i in range(2):
         row = slice(i, i + 1)
@@ -230,13 +220,11 @@
     each_chunk(meta, 1, grads)
 
 
-def third_pass(meta, vec, lse, q_ref, g_ref, dq_in, own_hbm, dq_ref, dkv, kv, q_st, g_st, dq, sem):
-    copy = fetch_all(own_hbm, kv, sem)
+def third_pass(meta, vec, lse, q_ref, g_ref, dq_in, kv, dq_ref, dkv, q_st, g_st, dq):
     dkv[...] = jnp.zeros_like(dkv)
     dq[...] = dq_in[...]
     for i in range(2):
         q_st[i], g_st[i] = stacked(q_ref, i), stacked(g_ref, i)
-    copy.wait()
 
     def grads(ch, i):
         keys = load(kv, meta, 0, ch, KEYS)
@@ -254,7 +242,6 @@
 
 SMEM = pl.BlockSpec(memory_space=pltpu.SMEM)
 VMEM = pl.BlockSpec(memory_space=pltpu.VMEM)
-ANY = pl.BlockSpec(memory_space=pl.ANY)
 
 
 def shape(*dims, dtype=jnp.bfloat16):
@@ -268,7 +255,7 @@
         in_specs=ins,
         out_specs=out_specs,
         scratch_shapes=scratch,
-        compiler_params=pltpu.CompilerParams(vmem_limit_bytes=48 * 1024 * 1024),
+        compiler_params=pltpu.CompilerParams(vmem_limit_bytes=24 * 1024 * 1024),
         cost_estimate=pl.CostEstimate(flops=flops, bytes_accessed=size, transcendentals=0),
         name=name,
     )
@@ -278,16 +265,16 @@
     tokens = queries.shape[0]
     f32, i32, bf16 = jnp.float32, jnp.int32, jnp.bfloat16
     plane = HALF * BLK
-    padded = pltpu.VMEM((plane, 2 * HD), bf16)
     scores = pltpu.VMEM((LIST * BLK, LANES), f32)
     weights = pltpu.VMEM((LIST * BLK, LANES), bf16)
     rows = pltpu.VMEM((2, LANES, HD), bf16)
     pair = pltpu.VMEM((2, LANES), f32)
     sums = pltpu.VMEM((2, HD, LANES), f32)
-    sem = pltpu.SemaphoreType.DMA
     kv = jnp.concatenate([key_rows, value_rows], axis=1)
     kv = (kv.astype(f32) * LIFT).astype(jnp.float16)
-    line = lax.all_gather(kv, "ctx", axis=0, tiled=True, axis_index_groups=FIRST)
+    line = jnp.broadcast_to(kv[None], (SIDE, tokens, 2 * HD))
+    line = lax.all_to_all(line, "ctx", 0, 0, tiled=True, axis_index_groups=FIRST)
+    line = line.reshape(SIDE * tokens, 2 * HD)
     own = lax.all_gather(line, "ctx", axis=0, tiled=True, axis_index_groups=SECOND)
     own = (own.astype(f32) * (1 / LIFT)).astype(bf16)
     oth = lax.ppermute(own, "ctx", SWAP)
@@ -296,20 +283,20 @@
     meta, vec, stat, part = kernel(
         first_pass,
         "forward_own",
-        [SMEM, SMEM, VMEM, ANY],
+        [SMEM, SMEM, VMEM, VMEM],
         (shape(META, dtype=i32), shape(4, LANES, dtype=i32), small, wide),
         (SMEM, VMEM, VMEM, VMEM),
-        [padded, rows, scores, pair, pair, pltpu.SMEM((NBLK,), i32), sem],
+        [rows, scores, pair, pair, pltpu.SMEM((NBLK,), i32)],
         2 * 10**9,
         4 * 10**6,
     )(block_order, doc_lengths, queries, own)
     attention, lse, dq, dkv_oth = kernel(
         second_pass,
         "other_plane",
-        [SMEM, VMEM, VMEM, VMEM, VMEM, VMEM, ANY],
+        [SMEM, VMEM, VMEM, VMEM, VMEM, VMEM, VMEM],
         (shape(tokens, 2 * HD), small, wide, shape(plane, 2 * HD)),
         (VMEM,) * 4,
-        [padded, rows, rows, rows, scores, weights, pair, pair, sums, pair, sem],
+        [rows, rows, rows, scores, weights, pair, pair, sums, pair],
         4 * 10**9,
         6 * 10**6,
     )(meta, vec, stat, queries, grad_output, part, oth)
@@ -317,10 +304,10 @@
     grad_queries, dkv_own = kernel(
         third_pass,
         "backward_own",
-        [SMEM, VMEM, VMEM, VMEM, VMEM, VMEM, ANY],
+        [SMEM, VMEM, VMEM, VMEM, VMEM, VMEM, VMEM],
         (shape(tokens, 2 * HD), shape(plane, 2 * HD)),
         (VMEM,) * 2,
-        [padded, rows, rows, sums, sem],
+        [rows, rows, sums],
         3 * 10**9,
         6 * 10**6,
     )(meta, vec, lse, queries, grad_output, dq, own)

time: 79.2 us -> 76.7 us (0.968)
  blocking collectives: 60.9 us -> 59.2 us
  waiting for transfers between devices: 0.81 us -> 1.77 us
    all_gather x1 -> x0, blocking collectives: 13.3 us -> none  [per_device(): lax.all_gather(kv, 'ctx', axis=0, tiled=True, axis_index_groups=FIRST)]
    all_to_all x0 -> x1, blocking collectives: none -> 12.3 us  [per_device(): lax.all_to_all(line, 'ctx', 0, 0, tiled=True, axis_index_groups=FIRST)]
    all_to_all x1, blocking collectives: 12.3 us -> 10.6 us  [per_device(): lax.all_to_all(part, 'ctx', 0, 0, tiled=True, axis_index_groups=FIRST)]
    all_to_all x1, blocking collectives: 19 us -> 20 us  [per_device(): lax.all_to_all(part, 'ctx', 0, 0, tiled=True, axis_index_groups=SECOND)]
  transfers between devices with their start and end apart: 2 -> 2, of which waited for: 2 -> 2; matrix products, arithmetic and copies ran while one was open for 0% -> 0% of each run, Pallas kernels for 9% -> 8%
where the time goes in v6:
time: 76.7 us; the launch traced here: 75.9 us
  blocking collectives  59.2 us (77%)
  Pallas kernels  9.3 us (12%)
  other arithmetic  2.81 us (4%)
  waiting for transfers between devices  1.77 us (2%)
  starting transfers between devices  1.26 us (2%)
  local copies, waits for them, and re-layouts  0.93 us (1%)
    all_to_all x1, blocking collectives, per_device(): lax.all_to_all(part, 'ctx', 0, 0, tiled=True, axis_index_groups=SECOND)  20 us
    all_gather x1, blocking collectives, per_device(): lax.all_gather(line, 'ctx', axis=0, tiled=True, axis_index_groups=SECOND)  16.3 us
    all_to_all x1, blocking collectives, per_device(): lax.all_to_all(line, 'ctx', 0, 0, tiled=True, axis_index_groups=FIRST)  12.3 us
    all_to_all x1, blocking collectives, per_device(): lax.all_to_all(part, 'ctx', 0, 0, tiled=True, axis_index_groups=FIRST)  10.6 us
    pallas_call x1, Pallas kernels, per_device(): kernel(second_pass, 'other_plane', [SMEM, VMEM, VMEM, VMEM, VMEM, VMEM, V...  3.36 us
    pallas_call x1, Pallas kernels, per_device(): kernel(third_pass, 'backward_own', [SMEM, VMEM, VMEM, VMEM, VMEM, VMEM, V...  3.07 us
    pallas_call x1, Pallas kernels, per_device(): kernel(first_pass, 'forward_own', [SMEM, SMEM, VMEM, VMEM], (shape(META,...  2.87 us
  transfers between devices with their start and end apart: 2, of which 2 were waited for; matrix products, arithmetic and copies ran while one was open for 0% of the time, Pallas kernels for 8%

profile of v6, /device:TPU:160, one launch (start us, length us, event | category | flops | bytes accessed | tf_op | source)
XLA Modules:
  0.0 75.9 jit_solution(5713147312343787070)
XLA Ops:
  0.6 0.9 %multiply_convert_fusion.1 = f16[256,256]{1,0:T(8,128)(2,1)S(1)} fusion(bf16[256,128]{1,0:T(8,128)(2,1)} %param.8, bf16[256,128]{1,0:T(8,128)(2,1)} %param.7), kind=kLoop, calls=%fused_computation.2 | loop fusion | flops 393216 | bytes 262144 | tf_op jit(solution)/shard_map/convert_element_type | solution.py:274
  1.6 12.3 %all_to_all.15 = f16[4,256,256]{2,1,0:T(8,128)(2,1)S(1)} all-to-all(f16[4,256,256]{2,1,0:T(8,128)(2,1)S(1)} %broadcast_in_dim.2), channel_id=1, replica_groups={{0,8,16,24},{2,10,18,26},{4,12,20,28},{6,14,22,30},{1,3,5,7},{9,11,13,1..., dimensions={0} | all-to-all | bytes 1048576 | tf_op jit(solution)/shard_map/all_to_all | solution.py:276
  13.9 16.3 %all-gather.1 = f16[4096,256]{1,0:T(8,128)(2,1)S(1)} all-gather(f16[1024,256]{1,0:T(8,128)(2,1)S(1)} %bitcast.4), channel_id=1, replica_groups={{0,2,4,6},{8,10,12,14},{16,18,20,22},{24,26,28,30},{1,9,17,25},{3,11,19..., dimensions={0}, use_global_device_ids=true | all-gather | bytes 2621440 | tf_op jit(solution)/shard_map/all_gather | solution.py:278
  30.2 0.0 copy-start
  30.2 0.0 copy-start.2
  30.2 0.0 copy-start.3
  30.2 0.6 multiply_convert_fusion.kv
  30.8 0.0 copy-start.1
  30.8 0.1 collective-permute-start
  30.9 0.2 copy-done
  31.1 0.0 copy-done.2
  31.1 0.0 copy-done.3
  31.1 2.9 %forward_own.1 = (s32[256]{0:T(256)S(1)}, s32[4,256]{1,0:T(4,128)S(1)}, f32[4,256]{1,0:T(4,128)S(1)}, f32[2,128,256]{2,1,0:T(8,128)S(1)}) custom-call(s32[64]{0:T(128)S(1)} %copy-done.2, s32[16]{0:T(128)S(1)} %copy-done.3, bf16[256,256]{1,0:T(8,128)(2,1)S(1)} %copy-done, bf16[4096,256]{1,0:T(8,128)(2,1)S(1)} %multiply_convert_fusion.kv), custom_call_target="tpu_custom_call" | custom-call | flops 2000000000 | bytes 4000000 | tf_op jit(solution)/shard_map/forward_own/pallas_call | solution.py:283
  34.0 1.1 %collective-permute-done.kv = bf16[4096,256]{1,0:T(8,128)(2,1)S(1)} collective-permute-done((bf16[4096,256]{1,0:T(8,128)(2,1)S(1)}, bf16[4096,256]{1,0:T(8,128)(2,1)S(1)}, u32[]{:S(2)}, u32[]{:S(2)}) %collective-permute-start) | collective-permute-done | bytes 2097184 | tf_op jit(solution)/shard_map/ppermute | solution.py:280
  35.1 0.0 copy-done.1
  35.1 3.4 %other_plane.1 = (bf16[256,256]{1,0:T(8,128)(2,1)}, f32[4,256]{1,0:T(4,128)S(1)}, f32[2,128,256]{2,1,0:T(8,128)S(1)}, bf16[4096,256]{1,0:T(8,128)(2,1)S(1)}) custom-call(s32[256]{0:T(256)S(1)} %get-tuple-element.14.meta, s32[4,256]{1,0:T(4,128)S(1)} %get-tuple-element.15.vec, f32[4,256]{1,0:T(4,128)S(1)} %get-tuple-element.16.stat, ...), custom_call_target="tpu_custom_call" | custom-call | flops 4000000000 | bytes 6000000 | tf_op jit(solution)/shard_map/other_plane/pallas_call | solution.py:293
  38.4 1.2 %collective-permute-start.1 = (bf16[4096,256]{1,0:T(8,128)(2,1)S(1)}, bf16[4096,256]{1,0:T(8,128)(2,1)S(1)}, u32[]{:S(2)}, u32[]{:S(2)}) collective-permute-start(bf16[4096,256]{1,0:T(8,128)(2,1)S(1)} %get-tuple-element.23), channel_id=1, source_target_pairs={{0,1},{1,0},{2,3},{3,2},{4,5},{5,4},{6,7},{7,6},{8,9},{9,8},{10,11... | collective-permute-start | bytes 6291464 | tf_op jit(solution)/shard_map/ppermute | solution.py:303
  39.6 3.1 %backward_own.1 = (bf16[256,256]{1,0:T(8,128)(2,1)}, bf16[4096,256]{1,0:T(8,128)(2,1)S(1)}) custom-call(s32[256]{0:T(256)S(1)} %get-tuple-element.14.meta, s32[4,256]{1,0:T(4,128)S(1)} %get-tuple-element.15.vec, f32[4,256]{1,0:T(4,128)S(1)} %get-tuple-element.19.lse, bf16[256,256]{1,0:T(8,128)(2,1)S(1)} %copy-done, bf16[256,256]{1,0:T(8,128)(2,1)S(1)} %copy-done.1, ...), custom_call_target="tpu_custom_call" | custom-call | flops 3000000000 | bytes 6000000 | tf_op jit(solution)/shard_map/backward_own/pallas_call | solution.py:304
  42.7 0.7 collective-permute-done.1
  43.4 0.6 add_convert_fusion
  44.0 20.0 %all_to_all.16 = bf16[4,1024,256]{2,1,0:T(8,128)(2,1)S(1)} all-to-all(bf16[4,1024,256]{2,1,0:T(8,128)(2,1)S(1)} %bitcast.3), channel_id=1, replica_groups={{0,2,4,6},{8,10,12,14},{16,18,20,22},{24,26,28,30},{1,9,17,25},{3,11,19..., dimensions={0} | all-to-all | bytes 4194304 | tf_op jit(solution)/shard_map/all_to_all | solution.py:316
  64.0 0.6 reduce_sum.24
  64.6 10.6 %all_to_all.17 = bf16[4,256,256]{2,1,0:T(8,128)(2,1)S(1)} all-to-all(bf16[4,256,256]{2,1,0:T(8,128)(2,1)S(1)} %bitcast.5), channel_id=1, replica_groups={{0,8,16,24},{2,10,18,26},{4,12,20,28},{6,14,22,30},{1,3,5,7},{9,11,13,1..., dimensions={0} | all-to-all | bytes 1048576 | tf_op jit(solution)/shard_map/all_to_all | solution.py:318
  75.2 0.1 reduce_sum.25
  75.3 0.7 fusion
  (1 shorter events, 0.0 us)
Async XLA Ops:
  30.2 0.9 %copy-start = (bf16[256,256]{1,0:T(8,128)(2,1)S(1)}, bf16[256,256]{1,0:T(8,128)(2,1)}, u32[]{:S(2)}) copy-start(bf16[256,256]{1,0:T(8,128)(2,1)} %q_ref.5) | copy-start | bytes 393220
  30.2 0.9 %copy-start.2 = (s32[64]{0:T(128)S(1)}, s32[64]{0:T(128)}, u32[]{:S(2)}) copy-start(s32[64]{0:T(128)} %order.1) | copy-start | bytes 772
  30.2 0.9 %copy-start.3 = (s32[16]{0:T(128)S(1)}, s32[16]{0:T(128)}, u32[]{:S(2)}) copy-start(s32[16]{0:T(128)} %lengths.1) | copy-start | bytes 196
  30.8 4.3 %copy-start.1 = (bf16[256,256]{1,0:T(8,128)(2,1)S(1)}, bf16[256,256]{1,0:T(8,128)(2,1)}, u32[]{:S(2)}) copy-start(bf16[256,256]{1,0:T(8,128)(2,1)} %g_ref.3) | copy-start | bytes 393220
  30.8 4.2 %collective-permute-start = (bf16[4096,256]{1,0:T(8,128)(2,1)S(1)}, bf16[4096,256]{1,0:T(8,128)(2,1)S(1)}, u32[]{:S(2)}, u32[]{:S(2)}) collective-permute-start(bf16[4096,256]{1,0:T(8,128)(2,1)S(1)} %multiply_convert_fusion.kv), channel_id=1, source_target_pairs={{0,1},{1,0},{2,3},{3,2},{4,5},{5,4},{6,7},{7,6},{8,9},{9,8},{10,11... | collective-permute-start | bytes 6291464 | tf_op jit(solution)/shard_map/ppermute | solution.py:280
  38.4 5.0 %collective-permute-start.1 = (bf16[4096,256]{1,0:T(8,128)(2,1)S(1)}, bf16[4096,256]{1,0:T(8,128)(2,1)S(1)}, u32[]{:S(2)}, u32[]{:S(2)}) collective-permute-start(bf16[4096,256]{1,0:T(8,128)(2,1)S(1)} %get-tuple-element.23), channel_id=1, source_target_pairs={{0,1},{1,0},{2,3},{3,2},{4,5},{5,4},{6,7},{7,6},{8,9},{9,8},{10,11... | collective-permute-start | bytes 6291464 | tf_op jit(solution)/shard_map/ppermute | solution.py:303

commit v7 on v6

--- a/solution.py
+++ b/solution.py
@@ -220,7 +220,8 @@
     each_chunk(meta, 1, grads)
 
 
-def third_pass(meta, vec, lse, q_ref, g_ref, dq_in, kv, dq_ref, dkv, q_st, g_st, dq):
+def third_pass(meta, vec, lse, q_ref, g_ref, dq_in, att_in, kv, o_ref, dq_ref, dkv, q_st, g_st, dq):
+    o_ref[...] = att_in[...]
     dkv[...] = jnp.zeros_like(dkv)
     dq[...] = dq_in[...]
     for i in range(2):
@@ -290,7 +291,7 @@
         2 * 10**9,
         4 * 10**6,
     )(block_order, doc_lengths, queries, own)
-    attention, lse, dq, dkv_oth = kernel(
+    att, lse, dq, dkv_oth = kernel(
         second_pass,
         "other_plane",
         [SMEM, VMEM, VMEM, VMEM, VMEM, VMEM, VMEM],
@@ -301,16 +302,16 @@
         6 * 10**6,
     )(meta, vec, stat, queries, grad_output, part, oth)
     back = lax.ppermute(dkv_oth, "ctx", SWAP)
-    grad_queries, dkv_own = kernel(
+    attention, grad_queries, dkv_own = kernel(
         third_pass,
         "backward_own",
-        [SMEM, VMEM, VMEM, VMEM, VMEM, VMEM, VMEM],
-        (shape(tokens, 2 * HD), shape(plane, 2 * HD)),
-        (VMEM,) * 2,
+        [SMEM, VMEM, VMEM, VMEM, VMEM, VMEM, VMEM, VMEM],
+        (shape(tokens, 2 * HD), shape(tokens, 2 * HD), shape(plane, 2 * HD)),
+        (VMEM,) * 3,
         [rows, rows, sums],
         3 * 10**9,
         6 * 10**6,
-    )(meta, vec, lse, queries, grad_output, dq, own)
+    )(meta, vec, lse, queries, grad_output, dq, att, own)
     part = (dkv_own.astype(f32) + back.astype(f32)).astype(bf16)
     part = part.reshape(SIDE, SIDE * tokens, 2 * HD)
     part = lax.all_to_all(part, "ctx", 0, 0, tiled=True, axis_index_groups=SECOND)

time: 76.7 us -> 76.3 us (level)
  blocking collectives: 59.2 us -> 60.3 us
  starting transfers between devices: 1.26 us -> 0.32 us
    all_to_all x1, blocking collectives: 20 us -> 21.2 us  [per_device(): lax.all_to_all(part, 'ctx', 0, 0, tiled=True, axis_index_groups=SECOND)]
    ppermute x1, starting transfers between devices: 1.17 us -> 0.22 us  [per_device(): back = lax.ppermute(dkv_oth, 'ctx', SWAP)]
where the time goes in v7:
time: 76.3 us; the launch traced here: 75.7 us
  blocking collectives  60.3 us (79%)
  Pallas kernels  8.65 us (11%)
  other arithmetic  2.81 us (4%)
  waiting for transfers between devices  2 us (3%)
  local copies, waits for them, and re-layouts  0.93 us (1%)
    all_to_all x1, blocking collectives, per_device(): lax.all_to_all(part, 'ctx', 0, 0, tiled=True, axis_index_groups=SECOND)  21.2 us
    all_gather x1, blocking collectives, per_device(): lax.all_gather(line, 'ctx', axis=0, tiled=True, axis_index_groups=SECOND)  16.3 us
    all_to_all x1, blocking collectives, per_device(): lax.all_to_all(line, 'ctx', 0, 0, tiled=True, axis_index_groups=FIRST)  12.3 us
    all_to_all x1, blocking collectives, per_device(): lax.all_to_all(part, 'ctx', 0, 0, tiled=True, axis_index_groups=FIRST)  10.5 us
    pallas_call x1, Pallas kernels, per_device(): kernel(third_pass, 'backward_own', [SMEM, VMEM, VMEM, VMEM, VMEM, VMEM, V...  3.08 us
    pallas_call x1, Pallas kernels, per_device(): kernel(first_pass, 'forward_own', [SMEM, SMEM, VMEM, VMEM], (shape(META,...  2.87 us
    pallas_call x1, Pallas kernels, per_device(): kernel(second_pass, 'other_plane', [SMEM, VMEM, VMEM, VMEM, VMEM, VMEM, V...  2.7 us
  transfers between devices with their start and end apart: 2, of which 2 were waited for; matrix products, arithmetic and copies ran while one was open for 0% of the time, Pallas kernels for 8%

profile of v7, /device:TPU:160, one launch (start us, length us, event | category | flops | bytes accessed | tf_op | source)
XLA Modules:
  0.0 75.7 jit_solution(12159226871826366244)
XLA Ops:
  0.6 0.9 %multiply_convert_fusion.1 = f16[256,256]{1,0:T(8,128)(2,1)S(1)} fusion(bf16[256,128]{1,0:T(8,128)(2,1)} %param.8, bf16[256,128]{1,0:T(8,128)(2,1)} %param.7), kind=kLoop, calls=%fused_computation.2 | loop fusion | flops 393216 | bytes 262144 | tf_op jit(solution)/shard_map/convert_element_type | solution.py:275
  1.6 12.3 %all_to_all.15 = f16[4,256,256]{2,1,0:T(8,128)(2,1)S(1)} all-to-all(f16[4,256,256]{2,1,0:T(8,128)(2,1)S(1)} %broadcast_in_dim.2), channel_id=1, replica_groups={{0,8,16,24},{2,10,18,26},{4,12,20,28},{6,14,22,30},{1,3,5,7},{9,11,13,1..., dimensions={0} | all-to-all | bytes 1048576 | tf_op jit(solution)/shard_map/all_to_all | solution.py:277
  13.9 16.3 %all-gather.1 = f16[4096,256]{1,0:T(8,128)(2,1)S(1)} all-gather(f16[1024,256]{1,0:T(8,128)(2,1)S(1)} %bitcast.4), channel_id=1, replica_groups={{0,2,4,6},{8,10,12,14},{16,18,20,22},{24,26,28,30},{1,9,17,25},{3,11,19..., dimensions={0}, use_global_device_ids=true | all-gather | bytes 2621440 | tf_op jit(solution)/shard_map/all_gather | solution.py:279
  30.2 0.0 copy-start
  30.2 0.0 copy-start.2
  30.2 0.0 copy-start.3
  30.2 0.6 multiply_convert_fusion.kv
  30.8 0.0 copy-start.1
  30.8 0.1 collective-permute-start
  30.9 0.2 copy-done
  31.1 0.0 copy-done.2
  31.1 0.0 copy-done.3
  31.1 2.9 %forward_own.1 = (s32[256]{0:T(256)S(1)}, s32[4,256]{1,0:T(4,128)S(1)}, f32[4,256]{1,0:T(4,128)S(1)}, f32[2,128,256]{2,1,0:T(8,128)S(1)}) custom-call(s32[64]{0:T(128)S(1)} %copy-done.2, s32[16]{0:T(128)S(1)} %copy-done.3, bf16[256,256]{1,0:T(8,128)(2,1)S(1)} %copy-done, bf16[4096,256]{1,0:T(8,128)(2,1)S(1)} %multiply_convert_fusion.kv), custom_call_target="tpu_custom_call" | custom-call | flops 2000000000 | bytes 4000000 | tf_op jit(solution)/shard_map/forward_own/pallas_call | solution.py:284
  34.0 1.1 %collective-permute-done.kv = bf16[4096,256]{1,0:T(8,128)(2,1)S(1)} collective-permute-done((bf16[4096,256]{1,0:T(8,128)(2,1)S(1)}, bf16[4096,256]{1,0:T(8,128)(2,1)S(1)}, u32[]{:S(2)}, u32[]{:S(2)}) %collective-permute-start) | collective-permute-done | bytes 2097184 | tf_op jit(solution)/shard_map/ppermute | solution.py:281
  35.1 0.0 copy-done.1
  35.1 2.7 %other_plane.1 = (bf16[256,256]{1,0:T(8,128)(2,1)S(1)}, f32[4,256]{1,0:T(4,128)S(1)}, f32[2,128,256]{2,1,0:T(8,128)S(1)}, bf16[4096,256]{1,0:T(8,128)(2,1)S(1)}) custom-call(s32[256]{0:T(256)S(1)} %get-tuple-element.15.meta, s32[4,256]{1,0:T(4,128)S(1)} %get-tuple-element.16.vec, f32[4,256]{1,0:T(4,128)S(1)} %get-tuple-element.17.stat, ...), custom_call_target="tpu_custom_call" | custom-call | flops 4000000000 | bytes 6000000 | tf_op jit(solution)/shard_map/other_plane/pallas_call | solution.py:294
  37.8 0.2 collective-permute-start.1
  38.0 3.1 %backward_own.1 = (bf16[256,256]{1,0:T(8,128)(2,1)}, bf16[256,256]{1,0:T(8,128)(2,1)}, bf16[4096,256]{1,0:T(8,128)(2,1)S(1)}) custom-call(s32[256]{0:T(256)S(1)} %get-tuple-element.15.meta, s32[4,256]{1,0:T(4,128)S(1)} %get-tuple-element.16.vec, f32[4,256]{1,0:T(4,128)S(1)} %get-tuple-element.19.lse, bf16[256,256]{1,0:T(8,128)(2,1)S(1)} %copy-done, ...), custom_call_target="tpu_custom_call" | custom-call | flops 3000000000 | bytes 6000000 | tf_op jit(solution)/shard_map/backward_own/pallas_call | solution.py:305
  41.1 0.9 %collective-permute-done.1 = bf16[4096,256]{1,0:T(8,128)(2,1)S(1)} collective-permute-done((bf16[4096,256]{1,0:T(8,128)(2,1)S(1)}, bf16[4096,256]{1,0:T(8,128)(2,1)S(1)}, u32[]{:S(2)}, u32[]{:S(2)}) %collective-permute-start.1) | collective-permute-done | bytes 2097184 | tf_op jit(solution)/shard_map/ppermute | solution.py:304
  42.0 0.6 add_convert_fusion
  42.6 21.2 %all_to_all.16 = bf16[4,1024,256]{2,1,0:T(8,128)(2,1)S(1)} all-to-all(bf16[4,1024,256]{2,1,0:T(8,128)(2,1)S(1)} %bitcast.3), channel_id=1, replica_groups={{0,2,4,6},{8,10,12,14},{16,18,20,22},{24,26,28,30},{1,9,17,25},{3,11,19..., dimensions={0} | all-to-all | bytes 4194304 | tf_op jit(solution)/shard_map/all_to_all | solution.py:317
  63.9 0.6 reduce_sum.24
  64.5 10.5 %all_to_all.17 = bf16[4,256,256]{2,1,0:T(8,128)(2,1)S(1)} all-to-all(bf16[4,256,256]{2,1,0:T(8,128)(2,1)S(1)} %bitcast.5), channel_id=1, replica_groups={{0,8,16,24},{2,10,18,26},{4,12,20,28},{6,14,22,30},{1,3,5,7},{9,11,13,1..., dimensions={0} | all-to-all | bytes 1048576 | tf_op jit(solution)/shard_map/all_to_all | solution.py:319
  75.0 0.1 reduce_sum.25
  75.1 0.7 fusion
  (1 shorter events, 0.0 us)
Async XLA Ops:
  30.2 0.9 %copy-start = (bf16[256,256]{1,0:T(8,128)(2,1)S(1)}, bf16[256,256]{1,0:T(8,128)(2,1)}, u32[]{:S(2)}) copy-start(bf16[256,256]{1,0:T(8,128)(2,1)} %q_ref.5) | copy-start | bytes 393220
  30.2 0.9 %copy-start.2 = (s32[64]{0:T(128)S(1)}, s32[64]{0:T(128)}, u32[]{:S(2)}) copy-start(s32[64]{0:T(128)} %order.1) | copy-start | bytes 772
  30.2 0.9 %copy-start.3 = (s32[16]{0:T(128)S(1)}, s32[16]{0:T(128)}, u32[]{:S(2)}) copy-start(s32[16]{0:T(128)} %lengths.1) | copy-start | bytes 196
  30.8 4.3 %copy-start.1 = (bf16[256,256]{1,0:T(8,128)(2,1)S(1)}, bf16[256,256]{1,0:T(8,128)(2,1)}, u32[]{:S(2)}) copy-start(bf16[256,256]{1,0:T(8,128)(2,1)} %g_ref.3) | copy-start | bytes 393220
  30.8 4.2 %collective-permute-start = (bf16[4096,256]{1,0:T(8,128)(2,1)S(1)}, bf16[4096,256]{1,0:T(8,128)(2,1)S(1)}, u32[]{:S(2)}, u32[]{:S(2)}) collective-permute-start(bf16[4096,256]{1,0:T(8,128)(2,1)S(1)} %multiply_convert_fusion.kv), channel_id=1, source_target_pairs={{0,1},{1,0},{2,3},{3,2},{4,5},{5,4},{6,7},{7,6},{8,9},{9,8},{10,11... | collective-permute-start | bytes 6291464 | tf_op jit(solution)/shard_map/ppermute | solution.py:281
  37.8 4.2 %collective-permute-start.1 = (bf16[4096,256]{1,0:T(8,128)(2,1)S(1)}, bf16[4096,256]{1,0:T(8,128)(2,1)S(1)}, u32[]{:S(2)}, u32[]{:S(2)}) collective-permute-start(bf16[4096,256]{1,0:T(8,128)(2,1)S(1)} %get-tuple-element.25), channel_id=1, source_target_pairs={{0,1},{1,0},{2,3},{3,2},{4,5},{5,4},{6,7},{7,6},{8,9},{9,8},{10,11... | collective-permute-start | bytes 6291464 | tf_op jit(solution)/shard_map/ppermute | solution.py:304

commit v8 on v7

--- a/solution.py
+++ b/solution.py
@@ -87,16 +87,18 @@
 def each_chunk(meta, plane, body):
     split, total = meta[COUNT_AT + 2 * plane], meta[COUNT_AT + 2 * plane + 1]
 
-    def pair(t, _):
-        for ch in (2 * t, 2 * t + 1):
-            body(ch, jnp.where(ch >= split, 1, 0))
+    def run(first, count):
+        for ch in range(count):
+            body(first + ch, jnp.where(first + ch >= split, 1, 0))
+
+    def trip(t, _):
+        run(4 * t, 4)
         return 0
 
-    lax.fori_loop(0, total >> 1, pair, 0)
-
-    @pl.when((total & 1) == 1)
-    def _():
-        body(total - 1, jnp.where(total > split, 1, 0))
+    lax.fori_loop(0, total >> 2, trip, 0)
+    rest = total & ~3
+    for count in range(1, 4):
+        pl.when((total & 3) == count)(lambda count=count: run(rest, count))
 
 
 def chunk_at(ch):

time: 76.3 us -> 76.2 us (level)
  Pallas kernels: 8.65 us -> 7.74 us
  waiting for transfers between devices: 2 us -> 2.87 us
  transfers between devices with their start and end apart: 2 -> 2, of which waited for: 2 -> 2; matrix products, arithmetic and copies ran while one was open for 0% -> 0% of each run, Pallas kernels for 8% -> 6%
where the time goes in v8:
time: 76.2 us; the launch traced here: 75.9 us
  blocking collectives  60 us (79%)
  Pallas kernels  7.74 us (10%)
  waiting for transfers between devices  2.87 us (4%)
  other arithmetic  2.81 us (4%)
  local copies, waits for them, and re-layouts  0.93 us (1%)
  starting transfers between devices  0.88 us (1%)
    all_to_all x1, blocking collectives, per_device(): lax.all_to_all(part, 'ctx', 0, 0, tiled=True, axis_index_groups=SECOND)  20.9 us
    all_gather x1, blocking collectives, per_device(): lax.all_gather(line, 'ctx', axis=0, tiled=True, axis_index_groups=SECOND)  16.3 us
    all_to_all x1, blocking collectives, per_device(): lax.all_to_all(line, 'ctx', 0, 0, tiled=True, axis_index_groups=FIRST)  12.3 us
    all_to_all x1, blocking collectives, per_device(): lax.all_to_all(part, 'ctx', 0, 0, tiled=True, axis_index_groups=FIRST)  10.5 us
    pallas_call x1, Pallas kernels, per_device(): kernel(second_pass, 'other_plane', [SMEM, VMEM, VMEM, VMEM, VMEM, VMEM, V...  2.9 us
    pallas_call x1, Pallas kernels, per_device(): kernel(third_pass, 'backward_own', [SMEM, VMEM, VMEM, VMEM, VMEM, VMEM, V...  2.48 us
    pallas_call x1, Pallas kernels, per_device(): kernel(first_pass, 'forward_own', [SMEM, SMEM, VMEM, VMEM], (shape(META,...  2.36 us
    ppermute x1, waiting for transfers between devices, per_device(): oth = lax.ppermute(own, 'ctx', SWAP)  1.56 us
  transfers between devices with their start and end apart: 2, of which 2 were waited for; matrix products, arithmetic and copies ran while one was open for 0% of the time, Pallas kernels for 6%

profile of v8, /device:TPU:160, one launch (start us, length us, event | category | flops | bytes accessed | tf_op | source)
XLA Modules:
  0.0 75.9 jit_solution(13235384517851397782)
XLA Ops:
  0.6 0.9 %multiply_convert_fusion.1 = f16[256,256]{1,0:T(8,128)(2,1)S(1)} fusion(bf16[256,128]{1,0:T(8,128)(2,1)} %param.8, bf16[256,128]{1,0:T(8,128)(2,1)} %param.7), kind=kLoop, calls=%fused_computation.2 | loop fusion | flops 393216 | bytes 262144 | tf_op jit(solution)/shard_map/convert_element_type | solution.py:277
  1.6 12.3 %all_to_all.15 = f16[4,256,256]{2,1,0:T(8,128)(2,1)S(1)} all-to-all(f16[4,256,256]{2,1,0:T(8,128)(2,1)S(1)} %broadcast_in_dim.2), channel_id=1, replica_groups={{0,8,16,24},{2,10,18,26},{4,12,20,28},{6,14,22,30},{1,3,5,7},{9,11,13,1..., dimensions={0} | all-to-all | bytes 1048576 | tf_op jit(solution)/shard_map/all_to_all | solution.py:279
  13.9 16.3 %all-gather.1 = f16[4096,256]{1,0:T(8,128)(2,1)S(1)} all-gather(f16[1024,256]{1,0:T(8,128)(2,1)S(1)} %bitcast.4), channel_id=1, replica_groups={{0,2,4,6},{8,10,12,14},{16,18,20,22},{24,26,28,30},{1,9,17,25},{3,11,19..., dimensions={0}, use_global_device_ids=true | all-gather | bytes 2621440 | tf_op jit(solution)/shard_map/all_gather | solution.py:281
  30.2 0.0 copy-start
  30.2 0.0 copy-start.2
  30.2 0.0 copy-start.3
  30.2 0.6 multiply_convert_fusion.kv
  30.8 0.0 copy-start.1
  30.8 0.1 collective-permute-start
  30.9 0.2 copy-done
  31.1 0.0 copy-done.2
  31.1 0.0 copy-done.3
  31.1 2.4 %forward_own.1 = (s32[256]{0:T(256)S(1)}, s32[4,256]{1,0:T(4,128)S(1)}, f32[4,256]{1,0:T(4,128)S(1)}, f32[2,128,256]{2,1,0:T(8,128)S(1)}) custom-call(s32[64]{0:T(128)S(1)} %copy-done.2, s32[16]{0:T(128)S(1)} %copy-done.3, bf16[256,256]{1,0:T(8,128)(2,1)S(1)} %copy-done, bf16[4096,256]{1,0:T(8,128)(2,1)S(1)} %multiply_convert_fusion.kv), custom_call_target="tpu_custom_call" | custom-call | flops 2000000000 | bytes 4000000 | tf_op jit(solution)/shard_map/forward_own/pallas_call | solution.py:286
  33.5 1.6 %collective-permute-done.kv = bf16[4096,256]{1,0:T(8,128)(2,1)S(1)} collective-permute-done((bf16[4096,256]{1,0:T(8,128)(2,1)S(1)}, bf16[4096,256]{1,0:T(8,128)(2,1)S(1)}, u32[]{:S(2)}, u32[]{:S(2)}) %collective-permute-start) | collective-permute-done | bytes 2097184 | tf_op jit(solution)/shard_map/ppermute | solution.py:283
  35.1 0.0 copy-done.1
  35.1 2.9 %other_plane.1 = (bf16[256,256]{1,0:T(8,128)(2,1)S(1)}, f32[4,256]{1,0:T(4,128)S(1)}, f32[2,128,256]{2,1,0:T(8,128)S(1)}, bf16[4096,256]{1,0:T(8,128)(2,1)S(1)}) custom-call(s32[256]{0:T(256)S(1)} %get-tuple-element.15.meta, s32[4,256]{1,0:T(4,128)S(1)} %get-tuple-element.16.vec, f32[4,256]{1,0:T(4,128)S(1)} %get-tuple-element.17.stat, ...), custom_call_target="tpu_custom_call" | custom-call | flops 4000000000 | bytes 6000000 | tf_op jit(solution)/shard_map/other_plane/pallas_call | solution.py:296
  38.0 0.8 %collective-permute-start.1 = (bf16[4096,256]{1,0:T(8,128)(2,1)S(1)}, bf16[4096,256]{1,0:T(8,128)(2,1)S(1)}, u32[]{:S(2)}, u32[]{:S(2)}) collective-permute-start(bf16[4096,256]{1,0:T(8,128)(2,1)S(1)} %get-tuple-element.25), channel_id=1, source_target_pairs={{0,1},{1,0},{2,3},{3,2},{4,5},{5,4},{6,7},{7,6},{8,9},{9,8},{10,11... | collective-permute-start | bytes 6291464 | tf_op jit(solution)/shard_map/ppermute | solution.py:306
  38.8 2.5 %backward_own.1 = (bf16[256,256]{1,0:T(8,128)(2,1)}, bf16[256,256]{1,0:T(8,128)(2,1)}, bf16[4096,256]{1,0:T(8,128)(2,1)S(1)}) custom-call(s32[256]{0:T(256)S(1)} %get-tuple-element.15.meta, s32[4,256]{1,0:T(4,128)S(1)} %get-tuple-element.16.vec, f32[4,256]{1,0:T(4,128)S(1)} %get-tuple-element.19.lse, bf16[256,256]{1,0:T(8,128)(2,1)S(1)} %copy-done, ...), custom_call_target="tpu_custom_call" | custom-call | flops 3000000000 | bytes 6000000 | tf_op jit(solution)/shard_map/backward_own/pallas_call | solution.py:307
  41.2 1.3 %collective-permute-done.1 = bf16[4096,256]{1,0:T(8,128)(2,1)S(1)} collective-permute-done((bf16[4096,256]{1,0:T(8,128)(2,1)S(1)}, bf16[4096,256]{1,0:T(8,128)(2,1)S(1)}, u32[]{:S(2)}, u32[]{:S(2)}) %collective-permute-start.1) | collective-permute-done | bytes 2097184 | tf_op jit(solution)/shard_map/ppermute | solution.py:306
  42.6 0.6 add_convert_fusion
  43.2 20.9 %all_to_all.16 = bf16[4,1024,256]{2,1,0:T(8,128)(2,1)S(1)} all-to-all(bf16[4,1024,256]{2,1,0:T(8,128)(2,1)S(1)} %bitcast.3), channel_id=1, replica_groups={{0,2,4,6},{8,10,12,14},{16,18,20,22},{24,26,28,30},{1,9,17,25},{3,11,19..., dimensions={0} | all-to-all | bytes 4194304 | tf_op jit(solution)/shard_map/all_to_all | solution.py:319
  64.0 0.6 reduce_sum.24
  64.7 10.5 %all_to_all.17 = bf16[4,256,256]{2,1,0:T(8,128)(2,1)S(1)} all-to-all(bf16[4,256,256]{2,1,0:T(8,128)(2,1)S(1)} %bitcast.5), channel_id=1, replica_groups={{0,8,16,24},{2,10,18,26},{4,12,20,28},{6,14,22,30},{1,3,5,7},{9,11,13,1..., dimensions={0} | all-to-all | bytes 1048576 | tf_op jit(solution)/shard_map/all_to_all | solution.py:321
  75.1 0.1 reduce_sum.25
  75.2 0.7 fusion
  (1 shorter events, 0.0 us)
Async XLA Ops:
  30.2 0.9 %copy-start = (bf16[256,256]{1,0:T(8,128)(2,1)S(1)}, bf16[256,256]{1,0:T(8,128)(2,1)}, u32[]{:S(2)}) copy-start(bf16[256,256]{1,0:T(8,128)(2,1)} %q_ref.5) | copy-start | bytes 393220
  30.2 0.9 %copy-start.2 = (s32[64]{0:T(128)S(1)}, s32[64]{0:T(128)}, u32[]{:S(2)}) copy-start(s32[64]{0:T(128)} %order.1) | copy-start | bytes 772
  30.2 0.9 %copy-start.3 = (s32[16]{0:T(128)S(1)}, s32[16]{0:T(128)}, u32[]{:S(2)}) copy-start(s32[16]{0:T(128)} %lengths.1) | copy-start | bytes 196
  30.8 4.3 %copy-start.1 = (bf16[256,256]{1,0:T(8,128)(2,1)S(1)}, bf16[256,256]{1,0:T(8,128)(2,1)}, u32[]{:S(2)}) copy-start(bf16[256,256]{1,0:T(8,128)(2,1)} %g_ref.3) | copy-start | bytes 393220
  30.8 4.2 %collective-permute-start = (bf16[4096,256]{1,0:T(8,128)(2,1)S(1)}, bf16[4096,256]{1,0:T(8,128)(2,1)S(1)}, u32[]{:S(2)}, u32[]{:S(2)}) collective-permute-start(bf16[4096,256]{1,0:T(8,128)(2,1)S(1)} %multiply_convert_fusion.kv), channel_id=1, source_target_pairs={{0,1},{1,0},{2,3},{3,2},{4,5},{5,4},{6,7},{7,6},{8,9},{9,8},{10,11... | collective-permute-start | bytes 6291464 | tf_op jit(solution)/shard_map/ppermute | solution.py:283
  38.0 4.6 %collective-permute-start.1 = (bf16[4096,256]{1,0:T(8,128)(2,1)S(1)}, bf16[4096,256]{1,0:T(8,128)(2,1)S(1)}, u32[]{:S(2)}, u32[]{:S(2)}) collective-permute-start(bf16[4096,256]{1,0:T(8,128)(2,1)S(1)} %get-tuple-element.25), channel_id=1, source_target_pairs={{0,1},{1,0},{2,3},{3,2},{4,5},{5,4},{6,7},{7,6},{8,9},{9,8},{10,11... | collective-permute-start | bytes 6291464 | tf_op jit(solution)/shard_map/ppermute | solution.py:306
